TPU v7x, 32 devices: a whole 2x2x4 slice. The times are simulated.
32 devices in a mesh: dp: 8 (over z, x), tensor: 4 (over y, core).
Axes of the slice: x: 2, y: 2, z: 4, core: 2. Of those that a mesh axis runs over, the one named last changes fastest.
Arguments:
- x_home: bfloat16 [16000, 1120], P('dp', 'tensor'), may hold values from -12 to 12
- cot_home: bfloat16 [16000, 1120], P('dp', 'tensor'), may hold values from -6 to 6
- cell_len: int32 [8, 4], replicated, may hold values from 128 to 500, as said below
- norm1_gain: float32 [1120], P('tensor'), may hold values from 0.1 to 1.9
- norm1_bias: float32 [1120], P('tensor'), may hold values from -3 to 3
- qkv_weight: bfloat16 [1120, 3, 1120], P(None, None, 'tensor'), may hold values from -0.1875 to 0.1875
- out_weight: bfloat16 [1120, 1120], P('tensor'), may hold values from -1 to 1
- norm2_gain: float32 [1120], P('tensor'), may hold values from 0.1 to 1.9
- norm2_bias: float32 [1120], P('tensor'), may hold values from -3 to 3
- up_weight: bfloat16 [1120, 4480], P(None, 'tensor'), may hold values from -0.1875 to 0.1875
- down_weight: bfloat16 [4480, 1120], P('tensor'), may hold values from -0.09375 to 0.09375
Outputs:
- out: bfloat16 [16000, 1120], P('dp', 'tensor')
- x_grad: bfloat16 [16000, 1120], P('dp', 'tensor')
- norm1_gain_grad: float32 [1120], P('tensor')
- norm1_bias_grad: float32 [1120], P('tensor')
- qkv_grad: float32 [1120, 3, 1120], P(None, None, 'tensor')
- out_grad: float32 [1120, 1120], P('tensor')
- norm2_gain_grad: float32 [1120], P('tensor')
- norm2_bias_grad: float32 [1120], P('tensor')
- up_grad: float32 [1120, 4480], P(None, 'tensor')
- down_grad: float32 [4480, 1120], P('tensor')
Inputs may be any that keep to these rules, and one draw needn't show every extreme that they name: `cell_len`: every slot holds a cell of 128 or more genes, and some cell has exactly 500. With the masks M = (2, 1, 4, 5) of the four slots, the cells of slot k of homes g XOR M_k, over k, add up to at most 1536 rows for every group g, and to exactly 1536 for some group.
All inputs are finite; a program needn't handle non-finite values.
Results may differ from a plain program's by a relative error of at most 0.013.
The roundings to bfloat16 on the way count: a program that leaves them out, or rounds other values in their place, can miss the bound.
Values may be sent and summed in bfloat16 or wider, within the bound.
No kernel may reach another device: no remote copies, remote signals or barrier semaphores. Data moves between devices by JAX's collectives and lax.ppermute only.
A program may use at most 256 MiB of HBM per device.

v0:
```python
import jax
import jax.numpy as jnp
from jax import lax
from jax.sharding import PartitionSpec as P

D = 1120
HD = 56
MAXLEN = 500
WORK = 1536


EPS = 1e-05


def block_rows(row_count):
    block_size = row_count
    while block_size > 1024 and block_size % 2 == 0:
        block_size = block_size // 2
    return block_size


def key_span(row_count, block_size):
    reach = (MAXLEN + 126) // 128 * 128
    return min(row_count, block_size + reach)


def key_window(arrays, first_row, block_size, width):
    row_count = arrays[0].shape[0]
    key_start = jnp.clip(first_row + block_size - width, 0, row_count - width)
    return (key_start, tuple((lax.dynamic_slice_in_dim(item, key_start, width) for item in arrays)))


def contract_rows(left, right):
    return lax.dot_general(
        left, right, (((0,), (0,)), ((), ())), preferred_element_type=jnp.float32
    )


def contract_cols(left, right):
    return lax.dot_general(
        left, right, (((1,), (1,)), ((), ())), preferred_element_type=jnp.float32
    )


def gelu_tanh(values):
    return jax.nn.gelu(values, approximate=True)


def plan_tables(cell_len):
    groups = cell_len.shape[0]
    slot_count = cell_len.shape[1]
    half_way = groups // 2
    slot_masks = jnp.array([2, 1, half_way, half_way + 1], jnp.int32)
    destinations = jnp.bitwise_xor(
        jnp.arange(groups, dtype=jnp.int32)[:, None], slot_masks[None, :]
    )
    slot_ids = jnp.arange(slot_count)
    in_len = cell_len[destinations, slot_ids[None, :]]
    in_off = jnp.cumsum(in_len, axis=1) - in_len
    return (slot_masks, destinations, in_off[destinations, slot_ids[None, :]])


def row_moments(values):
    totals = lax.psum((jnp.sum(values, axis=1), jnp.sum(values * values, axis=1)), "tensor")
    mean_row = totals[0] / D
    inv_std = lax.rsqrt(totals[1] / D - mean_row * mean_row + EPS)
    return ((values - mean_row[:, None]) * inv_std[:, None], inv_std)


def gather_normed(values):
    return lax.all_gather(values, "tensor", axis=1, tiled=True)


def sum_branch(partial_value):
    return lax.psum_scatter(partial_value, "tensor", scatter_dimension=1, tiled=True)


def gather_grad(values):
    return lax.all_gather(values, "tensor", axis=1, tiled=True)


def sum_input_grad(partial_value):
    return lax.psum_scatter(partial_value, "tensor", scatter_dimension=1, tiled=True)


def norm_back(grad_norm, normed, inv_std, gain):
    grad_hat = grad_norm * gain
    totals = lax.psum((jnp.sum(grad_hat, axis=1), jnp.sum(grad_hat * normed, axis=1)), "tensor")
    grad_in = inv_std[:, None] * (
        grad_hat - totals[0][:, None] / D - normed * (totals[1][:, None] / D)
    )
    return (grad_in, jnp.sum(grad_norm * normed, axis=0), jnp.sum(grad_norm, axis=0))


def masked_scores(query_block, key_block, cell_ids, key_cells, key_start, block_index, block_size):
    first_row = block_index * block_size
    cell_block = lax.dynamic_slice_in_dim(cell_ids, first_row, block_size)
    row_block = first_row + jnp.arange(block_size)
    positions = key_start + jnp.arange(key_block.shape[0])
    scores = jnp.einsum(
        "qhd,khd->hqk", query_block, key_block, preferred_element_type=jnp.float32
    ) * HD ** (-0.5)
    allowed = (cell_block[:, None] == key_cells[None, :]) & (
        positions[None, :] <= row_block[:, None]
    )
    return jnp.where(allowed[None], scores, -1e30)


def attend(queries, key_vals, values, cell_ids):
    row_count = queries.shape[0]
    head_count = queries.shape[1] // HD
    block_size = block_rows(row_count)
    block_count = row_count // block_size
    width = key_span(row_count, block_size)
    query_heads = queries.reshape(block_count, block_size, head_count, HD)
    key_heads = key_vals.reshape(row_count, head_count, HD)
    value_heads = values.reshape(row_count, head_count, HD)

    def one_block(block_index):
        query_block = lax.dynamic_index_in_dim(query_heads, block_index, 0, keepdims=False)
        key_start, (key_block, value_block, key_cells) = key_window(
            (key_heads, value_heads, cell_ids), block_index * block_size, block_size, width
        )
        scores = masked_scores(
            query_block, key_block, cell_ids, key_cells, key_start, block_index, block_size
        )
        row_max = jnp.max(scores, axis=2, keepdims=True)
        shifted = jnp.exp(scores - row_max)
        row_total = jnp.sum(shifted, axis=2, keepdims=True)
        weights = (shifted / row_total).astype(jnp.bfloat16)
        mixed_block = jnp.einsum(
            "hqk,khd->qhd", weights, value_block, preferred_element_type=jnp.float32
        )
        return (mixed_block.astype(jnp.bfloat16), (row_max + jnp.log(row_total))[..., 0])

    mixed_heads, log_sums = lax.map(one_block, jnp.arange(block_count))
    return (mixed_heads.reshape(row_count, head_count * HD), log_sums)


def attend_back(queries, key_vals, values, log_sums, grad_mixed, cell_ids):
    row_count = queries.shape[0]
    head_count = queries.shape[1] // HD
    block_size = block_rows(row_count)
    block_count = row_count // block_size
    width = key_span(row_count, block_size)
    query_heads = queries.reshape(block_count, block_size, head_count, HD)
    grad_heads = grad_mixed.reshape(block_count, block_size, head_count, HD)
    key_heads = key_vals.reshape(row_count, head_count, HD)
    value_heads = values.reshape(row_count, head_count, HD)

    def one_block(carry, block_index):
        grad_keys, grad_values = carry
        query_block = lax.dynamic_index_in_dim(query_heads, block_index, 0, keepdims=False)
        grad_block = lax.dynamic_index_in_dim(grad_heads, block_index, 0, keepdims=False)
        block_sums = lax.dynamic_index_in_dim(log_sums, block_index, 0, keepdims=False)
        key_start, (key_block, value_block, key_cells) = key_window(
            (key_heads, value_heads, cell_ids), block_index * block_size, block_size, width
        )
        scores = masked_scores(
            query_block, key_block, cell_ids, key_cells, key_start, block_index, block_size
        )
        probs = jnp.exp(scores - block_sums[:, :, None])
        value_part = lax.dynamic_slice_in_dim(grad_values, key_start, width) + jnp.einsum(
            "hqk,qhd->khd",
            probs.astype(jnp.bfloat16),
            grad_block,
            preferred_element_type=jnp.float32,
        )
        grad_values = lax.dynamic_update_slice_in_dim(grad_values, value_part, key_start, 0)
        grad_probs = jnp.einsum(
            "qhd,khd->hqk", grad_block, value_block, preferred_element_type=jnp.float32
        )
        row_delta = jnp.sum(probs * grad_probs, axis=2, keepdims=True)
        grad_scores = (probs * (grad_probs - row_delta) * HD ** (-0.5)).astype(jnp.bfloat16)
        grad_query = jnp.einsum(
            "hqk,khd->qhd", grad_scores, key_block, preferred_element_type=jnp.float32
        )
        key_part = lax.dynamic_slice_in_dim(grad_keys, key_start, width) + jnp.einsum(
            "hqk,qhd->khd", grad_scores, query_block, preferred_element_type=jnp.float32
        )
        grad_keys = lax.dynamic_update_slice_in_dim(grad_keys, key_part, key_start, 0)
        return ((grad_keys, grad_values), grad_query)

    zeros_start = jnp.zeros((row_count, head_count, HD), jnp.float32)
    (grad_keys, grad_values), grad_query = lax.scan(
        one_block, (zeros_start, zeros_start), jnp.arange(block_count)
    )
    return (
        grad_query.reshape(row_count, -1),
        grad_keys.reshape(row_count, -1),
        grad_values.reshape(row_count, -1),
    )


def forward(rows_in, cell_ids, params):
    gain_one, bias_one, w_qkv, w_out, gain_two, bias_two, w_up, w_down = params
    col_count = w_qkv.shape[2]
    normed1, inv_one = row_moments(rows_in)
    full_one = gather_normed((normed1 * gain_one + bias_one).astype(jnp.bfloat16))
    joined = jnp.dot(
        full_one, w_qkv.reshape(D, 3 * col_count), preferred_element_type=jnp.float32
    ).astype(jnp.bfloat16)
    queries = joined[:, :col_count]
    key_vals = joined[:, col_count : 2 * col_count]
    values = joined[:, 2 * col_count :]
    mixed, log_sums = attend(queries, key_vals, values, cell_ids)
    middle = rows_in + sum_branch(jnp.dot(mixed, w_out, preferred_element_type=jnp.float32))
    normed2, inv_two = row_moments(middle)
    full_two = gather_normed((normed2 * gain_two + bias_two).astype(jnp.bfloat16))
    hidden_pre = jnp.dot(full_two, w_up, preferred_element_type=jnp.float32)
    hidden = gelu_tanh(hidden_pre).astype(jnp.bfloat16)
    result = middle + sum_branch(jnp.dot(hidden, w_down, preferred_element_type=jnp.float32))
    stored = (
        normed1,
        inv_one,
        full_one,
        queries,
        key_vals,
        values,
        mixed,
        log_sums,
        normed2,
        inv_two,
        full_two,
        hidden_pre,
        hidden,
    )
    return (result, stored)


def backward(grad_out, cell_ids, params, stored):
    gain_one, bias_one, w_qkv, w_out, gain_two, bias_two, w_up, w_down = params
    (
        normed1,
        inv_one,
        full_one,
        queries,
        key_vals,
        values,
        mixed,
        log_sums,
        normed2,
        inv_two,
        full_two,
        hidden_pre,
        hidden,
    ) = stored
    col_count = w_qkv.shape[2]
    grad_full = gather_grad(grad_out.astype(jnp.bfloat16))
    grad_down = contract_rows(hidden, grad_full)
    grad_hidden = contract_cols(grad_full, w_down)
    gelu_pull = jax.vjp(gelu_tanh, hidden_pre)[1]
    grad_pre = gelu_pull(grad_hidden)[0].astype(jnp.bfloat16)
    grad_up = contract_rows(full_two, grad_pre)
    grad_norm_two = sum_input_grad(contract_cols(grad_pre, w_up))
    grad_mid_norm, grad_gain_two, grad_bias_two = norm_back(
        grad_norm_two, normed2, inv_two, gain_two
    )
    grad_middle = grad_out + grad_mid_norm
    grad_full_mid = gather_grad(grad_middle.astype(jnp.bfloat16))
    grad_w_out = contract_rows(mixed, grad_full_mid)
    grad_mixed = contract_cols(grad_full_mid, w_out).astype(jnp.bfloat16)
    grad_query, grad_keys, grad_values = attend_back(
        queries, key_vals, values, log_sums, grad_mixed, cell_ids
    )
    grad_joined = jnp.concatenate([grad_query, grad_keys, grad_values], axis=1).astype(jnp.bfloat16)
    grad_qkv = contract_rows(full_one, grad_joined).reshape(D, 3, col_count)
    grad_norm_one = sum_input_grad(contract_cols(grad_joined, w_qkv.reshape(D, 3 * col_count)))
    grad_in_norm, grad_gain_one, grad_bias_one = norm_back(
        grad_norm_one, normed1, inv_one, gain_one
    )
    grad_in = grad_middle + grad_in_norm
    return (
        grad_in,
        (
            grad_gain_one,
            grad_bias_one,
            grad_qkv,
            grad_w_out,
            grad_gain_two,
            grad_bias_two,
            grad_up,
            grad_down,
        ),
    )


def run_layer(rows_in, grad_out, cell_ids, params):
    result, stored = forward(rows_in, cell_ids, params)
    inputs_again = lax.optimization_barrier((rows_in, result))[0]
    stored = forward(inputs_again, cell_ids, params)[1]
    grad_in, grads = backward(grad_out, cell_ids, params, stored)
    return (result, grad_in, grads)


def shards(
    x_home,
    cot_home,
    cell_len,
    norm1_gain,
    norm1_bias,
    qkv_weight,
    out_weight,
    norm2_gain,
    norm2_bias,
    up_weight,
    down_weight,
):
    params = (
        norm1_gain,
        norm1_bias,
        qkv_weight,
        out_weight,
        norm2_gain,
        norm2_bias,
        up_weight,
        down_weight,
    )
    groups = cell_len.shape[0]
    slot_count = cell_len.shape[1]
    home_rows = x_home.shape[0]
    col_count = x_home.shape[1]
    slot_masks, dest_table, off_table = plan_tables(cell_len)
    own_index = lax.axis_index("dp")
    my_len = lax.dynamic_index_in_dim(cell_len, own_index, 0, keepdims=False)
    my_dest = lax.dynamic_index_in_dim(dest_table, own_index, 0, keepdims=False)
    my_start = jnp.cumsum(my_len) - my_len
    home_pos = jnp.arange(home_rows)[:, None]
    inside = (home_pos >= my_start[None, :]) & (home_pos < (my_start + my_len)[None, :])
    home_live = jnp.any(inside, axis=1)
    weight = groups / jnp.sum(cell_len).astype(jnp.float32)
    zero_half = jnp.zeros((), jnp.bfloat16)
    slot_rows = jnp.arange(MAXLEN)
    target = jnp.arange(groups)
    match_dest = (my_dest[None, :] == target[:, None]) & (my_len[None, :] > 0)
    send_start = jnp.sum(jnp.where(match_dest, my_start[None, :], 0), axis=1)
    send_len = jnp.sum(jnp.where(match_dest, my_len[None, :], 0), axis=1)
    send_pick = jnp.minimum(send_start[:, None] + slot_rows[None, :], home_rows - 1).reshape(-1)
    send_live = (slot_rows[None, :] < send_len[:, None])[:, :, None]
    sent_rows = jnp.where(
        send_live, jnp.take(x_home, send_pick, axis=0).reshape(groups, MAXLEN, col_count), zero_half
    )
    sent_grads = jnp.where(
        send_live,
        jnp.take(cot_home, send_pick, axis=0).reshape(groups, MAXLEN, col_count),
        zero_half,
    )
    got_rows, got_grads = (
        lax.all_to_all(sent_rows, "dp", split_axis=0, concat_axis=0, tiled=True),
        lax.all_to_all(sent_grads, "dp", split_axis=0, concat_axis=0, tiled=True),
    )
    flat_len = cell_len.reshape(-1)
    flat_dest = dest_table.reshape(-1)
    flat_off = off_table.reshape(-1)
    to_me = (flat_dest == own_index) & (flat_len > 0)
    work_pos = jnp.arange(WORK)[:, None]
    cover = (
        to_me[None, :]
        & (work_pos >= flat_off[None, :])
        & (work_pos < (flat_off + flat_len)[None, :])
    )
    cell_index = jnp.arange(groups * slot_count)
    source_base = cell_index // slot_count * MAXLEN - flat_off
    recv_index = jnp.sum(jnp.where(cover, source_base[None, :] + work_pos + 1, 0), axis=1) - 1
    work_cells = jnp.sum(jnp.where(cover, cell_index[None, :] + 1, 0), axis=1) - 1
    work_live = (recv_index >= 0)[:, None]
    safe_rows = jnp.maximum(recv_index, 0)
    rows_in = jnp.where(
        work_live,
        jnp.take(got_rows.reshape(-1, col_count), safe_rows, axis=0).astype(jnp.float32),
        0.0,
    )
    grad_out = jnp.where(
        work_live,
        jnp.take(got_grads.reshape(-1, col_count), safe_rows, axis=0).astype(jnp.float32),
        0.0,
    )
    result, grad_in, grads = run_layer(rows_in, grad_out, work_cells, params)
    match_back = to_me.reshape(groups, slot_count)
    back_start = jnp.sum(jnp.where(match_back, off_table, 0), axis=1)
    back_len = jnp.sum(jnp.where(match_back, cell_len, 0), axis=1)
    back_pick = jnp.minimum(back_start[:, None] + slot_rows[None, :], WORK - 1).reshape(-1)
    back_live = (slot_rows[None, :] < back_len[:, None])[:, :, None]
    back_rows = jnp.where(
        back_live,
        jnp.take(result.astype(jnp.bfloat16), back_pick, axis=0).reshape(groups, MAXLEN, col_count),
        zero_half,
    )
    back_grads = jnp.where(
        back_live,
        jnp.take(grad_in.astype(jnp.bfloat16), back_pick, axis=0).reshape(
            groups, MAXLEN, col_count
        ),
        zero_half,
    )
    home_out, home_grad = (
        lax.all_to_all(back_rows, "dp", split_axis=0, concat_axis=0, tiled=True),
        lax.all_to_all(back_grads, "dp", split_axis=0, concat_axis=0, tiled=True),
    )
    home_index = (
        jnp.sum(
            jnp.where(inside, my_dest[None, :] * MAXLEN + home_pos - my_start[None, :] + 1, 0),
            axis=1,
        )
        - 1
    )
    safe_home = jnp.maximum(home_index, 0)
    out_rows = jnp.where(
        home_live[:, None], jnp.take(home_out.reshape(-1, col_count), safe_home, axis=0), zero_half
    )
    grad_rows = jnp.where(
        home_live[:, None], jnp.take(home_grad.reshape(-1, col_count), safe_home, axis=0), zero_half
    )
    summed = lax.psum(
        (grads[0], grads[1], grads[2], grads[3], grads[4], grads[5], grads[6], grads[7]), "dp"
    )
    scaled = tuple((item * weight for item in summed))
    return (out_rows, grad_rows) + scaled


def solution(mesh):
    placed = (
        P("dp", "tensor"),
        P("dp", "tensor"),
        P(),
        P("tensor"),
        P("tensor"),
        P(None, None, "tensor"),
        P("tensor", None),
        P("tensor"),
        P("tensor"),
        P(None, "tensor"),
        P("tensor", None),
    )
    return jax.shard_map(
        shards,
        mesh=mesh,
        in_specs=placed,
        out_specs=(
            P("dp", "tensor"),
            P("dp", "tensor"),
            P("tensor"),
            P("tensor"),
            P(None, None, "tensor"),
            P("tensor", None),
            P("tensor"),
            P("tensor"),
            P(None, "tensor"),
            P("tensor", None),
        ),
        check_vma=False,
    )
```

profile of v0, /device:TPU:0, one launch (start us, length us, event | category | flops | bytes accessed | tf_op | source)
XLA Modules:
  0.0 1780.5 jit_solution(10395259841289763374)
XLA Ops:
  18.5 18.3 %gather_fusion.2 = bf16[4000,280]{1,0:T(8,128)(2,1)} fusion(bf16[2000,280]{1,0:T(8,128)(2,1)} %copy.104, s32[4096]{0:T(1024)S(1)} %pad_clamp_fusion.1), kind=kCustom, calls=%fused_computation.clone | custom fusion | bytes 4496000 | tf_op jit(solution)/shard_map/jit(_take)/gather | solution.py:341
  36.8 18.3 %gather_fusion.6 = bf16[4000,280]{1,0:T(8,128)(2,1)} fusion(bf16[2000,280]{1,0:T(8,128)(2,1)} %copy.117, s32[4096]{0:T(1024)S(1)} %pad_clamp_fusion.1), kind=kCustom, calls=%fused_computation.4.clone | custom fusion | bytes 4496000 | tf_op jit(solution)/shard_map/jit(_take)/gather | solution.py:345
  97.2 52.0 %all-to-all-done = bf16[8,500,280]{1,2,0:T(8,128)(2,1)} async-done(((bf16[8,500,280]{1,2,0:T(8,128)(2,1)}), bf16[8,500,280]{1,2,0:T(8,128)(2,1)}, u32[]{:S(2)}, u32[]{:S(2)}) %all-to-all-start) | async-done | bytes 2240032 | tf_op jit(solution)/shard_map/all_to_all | solution.py:349
  179.6 29.2 %all-gather.7.cloned.1.call-done = bf16[1536,1120]{0,1:T(8,128)(2,1)} async-done(((bf16[1536,280]{0,1:T(8,128)(2,1)}), bf16[1536,1120]{0,1:T(8,128)(2,1)}) %all-gather.7.cloned.1.call-update) | async-done | bytes 3440656 | tf_op jit(solution)/shard_map/all_gather | solution.py:71
  219.7 50.3 %while.48 = (s32[]{:T(128)}, bf16[2,768,5,56]{1,3,2,0:T(8,128)(2,1)S(1)}, s32[2]{0:T(128)S(1)}, bf16[1536,5,56]{0,2,1:T(8,128)(2,1)}, s32[1536]{0:T(1024)S(1)}, ...) while((s32[]{:T(128)}, ...), condition=%wide.region_15.18_spmd, body=%wide.region_12.17_spmd.sunk | while | flops 1698916608 | bytes 6472997 | solution.py:136
  233.3 11.5 fusion.232
  258.4 11.4 fusion.232
  278.4 58.3 %all_to_all.20 = bf16[8,500,280]{1,2,0:T(8,128)(2,1)} all-to-all(bf16[8,500,280]{1,2,0:T(8,128)(2,1)S(1)} %copy.119), channel_id=1, replica_groups=mesh['dp'=8,'tensor'=4] {'dp'}, dimensions={0} | all-to-all | bytes 4480000 | tf_op jit(solution)/shard_map/all_to_all | solution.py:350
  372.6 28.7 %all-gather.9.cloned.1.call-done = bf16[1536,1120]{0,1:T(8,128)(2,1)} async-done(((bf16[1536,280]{0,1:T(8,128)(2,1)}), bf16[1536,1120]{0,1:T(8,128)(2,1)}) %all-gather.9.cloned.1.call-update) | async-done | bytes 3440656 | tf_op jit(solution)/shard_map/all_gather | solution.py:71
  401.3 20.8 %fusion.121 = f32[1536,1120]{0,1:T(8,128)} fusion(bf16[1120,1120]{1,0:T(8,128)(2,1)} %param.36, bf16[1536,1120]{0,1:T(8,128)(2,1)} %all-gather.9.cloned.1.call-done, bf16[1120,1120]{1,0:T(8,128)(2,1)S(1)} %copy-done), kind=kOutput, calls=%fused_computation.126 | convolution fusion | flops 7722516480 | bytes 15339520 | tf_op jit(solution)/shard_map/dot_general | solution.py:212
  422.2 62.5 %reduce-scatter.8.cloned.1.call-done = f32[1536,280]{0,1:T(8,128)} async-done(((f32[1536,1120]{0,1:T(8,128)}), f32[1536,280]{0,1:T(8,128)}) %reduce-scatter.8.cloned.1.call-update) | async-done | bytes 1720336 | tf_op jit(solution)/shard_map/reduce_scatter | solution.py:75
  501.8 31.3 %all-gather.11.cloned.1.call-done = bf16[1536,1120]{0,1:T(8,128)(2,1)} async-done(((bf16[1536,280]{0,1:T(8,128)(2,1)}), bf16[1536,1120]{0,1:T(8,128)(2,1)}) %all-gather.11.cloned.1.call-update) | async-done | bytes 3440656 | tf_op jit(solution)/shard_map/all_gather | solution.py:71
  544.9 41.3 %while.49 = (s32[]{:T(128)}, bf16[2,768,5,56]{1,3,2,0:T(8,128)(2,1)}, f32[2,5,768]{2,1,0:T(8,128)S(1)}, s32[2]{0:T(128)S(1)}, bf16[1536,5,56]{0,2,1:T(8,128)(2,1...) while((s32[]{:T(128)}, ...), condition=%wide.region_31.36_spmd, body=%wide.region_28.35_spmd.sunk | while | flops 1143488768 | bytes 63434040 | solution.py:136
  594.8 61.6 %reduce-scatter.10.cloned.1.call-done = f32[1536,280]{0,1:T(8,128)} async-done(((f32[1536,1120]{0,1:T(8,128)}), f32[1536,280]{0,1:T(8,128)}) %reduce-scatter.10.cloned.1.call-update) | async-done | bytes 1720336 | tf_op jit(solution)/shard_map/reduce_scatter | solution.py:75
  673.1 15.9 all-gather.13.cloned.1.call-done
  699.4 22.0 %all-gather.15.cloned.1.call-done = bf16[1536,1120]{0,1:T(8,128)(2,1)} async-done(((bf16[1536,280]{0,1:T(8,128)(2,1)}), bf16[1536,1120]{0,1:T(8,128)(2,1)}) %all-gather.15.cloned.1.call-update) | async-done | bytes 3440656 | tf_op jit(solution)/shard_map/all_gather | solution.py:71
  721.5 13.4 fusion.111
  743.4 62.4 %reduce-scatter.12.cloned.1.call-done = f32[1536,280]{0,1:T(8,128)} async-done(((f32[1536,1120]{0,1:T(8,128)}), f32[1536,280]{0,1:T(8,128)}) %reduce-scatter.12.cloned.1.call-update) | async-done | bytes 1720336 | tf_op jit(solution)/shard_map/reduce_scatter | solution.py:83
  825.4 31.3 %all-gather.17.cloned.1.call-done = bf16[1536,1120]{0,1:T(8,128)(2,1)} async-done(((bf16[1536,280]{0,1:T(8,128)(2,1)}), bf16[1536,1120]{0,1:T(8,128)(2,1)}) %all-gather.17.cloned.1.call-update) | async-done | bytes 3440656 | tf_op jit(solution)/shard_map/all_gather | solution.py:79
  867.2 199.2 %while.50 = (s32[]{:T(128)}, f32[1536,5,56]{0,2,1:T(8,128)}, f32[1536,5,56]{0,2,1:T(8,128)}, bf16[2,768,5,56]{1,3,2,0:T(8,128)(2,1)}, s32[2]{0:T(128)S(1)}, /*in...) while((s32[]{:T(128)}, f32[1536,5,56]{0,2,1:T(8,128)}, ...), condition=%wide.region_44.49_spmd, body=%wide.region_42.48_spmd.sunk | while | flops 2825003008 | bytes 320046528 | solution.py:185
  906.8 26.4 %fusion.250 = bf16[2,768,5,56]{1,3,2,0:T(8,128)(2,1)} fusion(bf16[2,768,5,56]{1,3,2,0:T(8,128)(2,1)} %get-tuple-element.1094, s32[]{:T(128)S(6)} %copy.171, f32[5,768,1280]{2,1,0:T(8,128)} %copy-done.2, f32[5,768,1280]{2,1,0:T(8,128)} %fusion.247, bf16[1536,5,56]{0,2,1:T(8,128)(2,1)} %get-tuple-element.1116, s32[]{:T(128)S(6)} %min.63), kind=kOutput, calls=%fused_computation.79.clone.1 | convolution fusion | flops 575083520 | bytes 80220168 | tf_op jit(solution)/shard_map/while/body/eval_jaxpr/hqk,khd->qhd/dot_general | solution.py:175
  933.2 27.2 %fusion.248 = f32[1280,5,56]{0,2,1:T(8,128)} fusion(f32[5,768,1280]{2,1,0:T(8,128)} %copy-done.2, f32[5,768,1280]{2,1,0:T(8,128)} %fusion.247, f32[1536,5,56]{0,2,1:T(8,128)} %get-tuple-element.1092, s32[]{:T(128)S(6)} %min.63, bf16[2,768,5,56]{1,3,2,0:T(8,128)(2,1)S(1)} %copy-done.18, s32[]{:T(128)S(6)} %select_n.374), kind=kOutput, calls=%fused_computation.75.clone.1 | convolution fusion | flops 575441920 | bytes 81940488 | tf_op jit(solution)/shard_map/while/body/eval_jaxpr/hqk,qhd->khd/dot_general | solution.py:178
  1006.1 26.4 %fusion.250 = bf16[2,768,5,56]{1,3,2,0:T(8,128)(2,1)} fusion(bf16[2,768,5,56]{1,3,2,0:T(8,128)(2,1)} %get-tuple-element.1094, s32[]{:T(128)S(6)} %copy.171, f32[5,768,1280]{2,1,0:T(8,128)} %copy-done.2, f32[5,768,1280]{2,1,0:T(8,128)} %fusion.247, bf16[1536,5,56]{0,2,1:T(8,128)(2,1)} %get-tuple-element.1116, s32[]{:T(128)S(6)} %min.63), kind=kOutput, calls=%fused_computation.79.clone.1 | convolution fusion | flops 575083520 | bytes 80220168 | tf_op jit(solution)/shard_map/while/body/eval_jaxpr/hqk,khd->qhd/dot_general | solution.py:175
  1032.5 27.2 %fusion.248 = f32[1280,5,56]{0,2,1:T(8,128)} fusion(f32[5,768,1280]{2,1,0:T(8,128)} %copy-done.2, f32[5,768,1280]{2,1,0:T(8,128)} %fusion.247, f32[1536,5,56]{0,2,1:T(8,128)} %get-tuple-element.1092, s32[]{:T(128)S(6)} %min.63, bf16[2,768,5,56]{1,3,2,0:T(8,128)(2,1)S(1)} %copy-done.18, s32[]{:T(128)S(6)} %select_n.374), kind=kOutput, calls=%fused_computation.75.clone.1 | convolution fusion | flops 575441920 | bytes 81940488 | tf_op jit(solution)/shard_map/while/body/eval_jaxpr/hqk,qhd->khd/dot_general | solution.py:178
  1087.7 12.3 fusion.120
  1110.9 18.3 %gather_fusion.4 = bf16[4000,280]{1,0:T(8,128)(2,1)} fusion(bf16[1536,280]{1,0:T(8,128)(2,1)} %copy.112, s32[4096]{0:T(1024)S(1)} %pad_clamp_fusion), kind=kCustom, calls=%fused_computation.2.clone | custom fusion | bytes 4496000 | tf_op jit(solution)/shard_map/jit(_take)/gather | solution.py:386
  1161.8 18.0 %gather_fusion.8 = bf16[4000,280]{1,0:T(8,128)(2,1)} fusion(bf16[1536,280]{1,0:T(8,128)(2,1)} %copy.128, s32[4096]{0:T(1024)S(1)} %pad_clamp_fusion), kind=kCustom, calls=%fused_computation.6.clone | custom fusion | bytes 4496000 | tf_op jit(solution)/shard_map/jit(_take)/gather | solution.py:391
  1226.3 84.8 %all-reduce = (f32[280]{0:T(512)S(1)}, f32[280]{0:T(512)S(1)}, f32[280]{0:T(512)S(1)}, f32[280]{0:T(512)S(1)}) all-reduce(f32[280]{0:T(512)S(1)} %get-tuple-element.689, f32[280]{0:T(512)S(1)} %get-tuple-element.696, f32[280]{0:T(512)S(1)} %copy-done.51, f32[280]{0:T(512)S(1)} %copy-done.52), channel_id=1, replica_groups=mesh['dp'=8,'tensor'=4] {'dp'}, use_global_device_ids=true, to_apply=%region_51.56 | all-reduce | flops 1120 | bytes 8960 | tf_op jit(solution)/shard_map/psum | solution.py:414
  1313.4 357.9 %all-reduce.10.cloned.1.call-done = (f32[1120,3,280]{0,2,1:T(8,128)}, f32[280,1120]{1,0:T(8,128)}, f32[1120,1120]{1,0:T(8,128)}, f32[1120,1120]{1,0:T(8,128)}) async-done(((f32[1120,3,280]{0,2,1:T(8,128)}, f32[280,1120]{1,0:T(8,128)}, f32[1120,1120]{1,0:T(8,128)}, f32[1120,1120]{1,0:T(8,128)}), (f32[1120,3,280]{0,2,1:T(8,128)}, f32[280,1120]{1,0:T(8,128)}, f32[1120,1120]{1,0:T(8,128)}, ...) | async-done | bytes 15052816 | tf_op jit(solution)/shard_map/psum | solution.py:414
  1699.8 33.1 %all-to-all-done.1 = bf16[8,500,280]{1,2,0:T(8,128)(2,1)} async-done(((bf16[8,500,280]{1,2,0:T(8,128)(2,1)}), bf16[8,500,280]{1,2,0:T(8,128)(2,1)}, u32[]{:S(2)}, u32[]{:S(2)}) %all-to-all-start.1) | async-done | bytes 2240032 | tf_op jit(solution)/shard_map/all_to_all | solution.py:397
  1742.1 11.1 gather_fusion.9
  1753.2 11.1 gather_fusion.5
  (383 shorter events, 544.3 us)
Async XLA Ops:
  7.2 394.1 %copy-start = (bf16[1120,1120]{1,0:T(8,128)(2,1)S(1)}, bf16[1120,1120]{1,0:T(8,128)(2,1)}, u32[]{:S(2)}) copy-start(bf16[1120,1120]{1,0:T(8,128)(2,1)} %param.35) | copy-start | bytes 7526404
  89.4 59.8 %all-to-all-start = ((bf16[8,500,280]{1,2,0:T(8,128)(2,1)}), bf16[8,500,280]{1,2,0:T(8,128)(2,1)}, u32[]{:S(2)}, u32[]{:S(2)}) async-start(bf16[8,500,280]{1,2,0:T(8,128)(2,1)} %copy.106), calls=%async_computation | async-start | bytes 4587520 | tf_op jit(solution)/shard_map/all_to_all | solution.py:349
  96.6 112.1 %all-gather.7.cloned.1.call-start = ((), (), s32[]{:S(2)}) async-start(), calls=%async_computation.9 | async-start | bytes 4300800 | tf_op jit(solution)/shard_map/all_gather | solution.py:71
  97.1 61.2 %copy-start.41 = (s32[2048]{0:T(1024)}, s32[2048]{0:T(1024)S(1)}, u32[]{:S(2)}) copy-start(s32[2048]{0:T(1024)S(1)} %pad_clamp_fusion.3) | copy-start | bytes 24580
  97.2 80.5 %copy-start.25 = (pred[1536]{0:T(1024)(128)(4,1)}, pred[1536]{0:T(1024)(128)(4,1)S(1)}, u32[]{:S(2)}) copy-start(pred[1536]{0:T(1024)(128)(4,1)S(1)} %get-tuple-element.801) | copy-start | bytes 4612
  97.2 80.5 %copy-start.29 = (pred[1536]{0:T(1024)(128)(4,1)}, pred[1536]{0:T(1024)(128)(4,1)S(1)}, u32[]{:S(2)}) copy-start(pred[1536]{0:T(1024)(128)(4,1)S(1)} %get-tuple-element.802) | copy-start | bytes 4612
  167.1 47.7 %copy-start.6 = (bf16[1536,280]{0,1:T(8,128)(2,1)}, bf16[1536,280]{0,1:T(8,128)(2,1)S(1)}, u32[]{:S(2)}) copy-start(bf16[1536,280]{0,1:T(8,128)(2,1)S(1)} %copy.109) | copy-start | bytes 2580484
  179.1 176.4 %reduce-scatter.6.cloned.1.call-start = ((), (), s32[]{:S(2)}) async-start(), calls=%async_computation.10 | async-start | bytes 8601600 | tf_op jit(solution)/shard_map/reduce_scatter | solution.py:75
  276.0 125.3 %all-gather.9.cloned.1.call-start = ((), (), s32[]{:S(2)}) async-start(), calls=%async_computation.11 | async-start | bytes 4300800 | tf_op jit(solution)/shard_map/all_gather | solution.py:71
  372.5 112.1 %reduce-scatter.8.cloned.1.call-start = ((), (), s32[]{:S(2)}) async-start(), calls=%async_computation.12 | async-start | bytes 8601600 | tf_op jit(solution)/shard_map/reduce_scatter | solution.py:75
  422.1 77.0 %copy-start.47 = (f32[280]{0:T(512)S(1)}, f32[280]{0:T(512)}, u32[]{:S(2)}) copy-start(f32[280]{0:T(512)} %param.29) | copy-start | bytes 3364
  422.1 77.0 %copy-start.50 = (f32[280]{0:T(512)S(1)}, f32[280]{0:T(512)}, u32[]{:S(2)}) copy-start(f32[280]{0:T(512)} %param.30) | copy-start | bytes 3364
  422.1 111.0 %all-gather.11.cloned.1.call-start = ((), (), s32[]{:S(2)}) async-start(), calls=%async_computation.13 | async-start | bytes 4300800 | tf_op jit(solution)/shard_map/all_gather | solution.py:71
  501.8 154.7 %reduce-scatter.10.cloned.1.call-start = ((), (), s32[]{:S(2)}) async-start(), calls=%async_computation.14 | async-start | bytes 8601600 | tf_op jit(solution)/shard_map/reduce_scatter | solution.py:75
  594.0 76.2 %copy-start.44 = (f32[280]{0:T(512)S(1)}, f32[280]{0:T(512)}, u32[]{:S(2)}) copy-start(f32[280]{0:T(512)} %param.33) | copy-start | bytes 3364
  594.0 76.2 %copy-start.56 = (f32[280]{0:T(512)S(1)}, f32[280]{0:T(512)}, u32[]{:S(2)}) copy-start(f32[280]{0:T(512)} %param.34) | copy-start | bytes 3364
  594.0 95.0 %all-gather.13.cloned.1.call-start = ((), (), s32[]{:S(2)}) async-start(), calls=%async_computation.15 | async-start | bytes 4300800 | tf_op jit(solution)/shard_map/all_gather | solution.py:79
  594.8 126.7 %all-gather.15.cloned.1.call-start = ((), (), s32[]{:S(2)}) async-start(), calls=%async_computation.16 | async-start | bytes 4300800 | tf_op jit(solution)/shard_map/all_gather | solution.py:71
  670.2 150.4 %copy-start.21 = (f32[1536]{0:T(1024)}, f32[1536]{0:T(1024)S(1)}, u32[]{:S(2)}) copy-start(f32[1536]{0:T(1024)S(1)} %get-tuple-element.793) | copy-start | bytes 18436
  670.2 150.4 %copy-start.23 = (f32[1536]{0:T(1024)}, f32[1536]{0:T(1024)S(1)}, u32[]{:S(2)}) copy-start(f32[1536]{0:T(1024)S(1)} %get-tuple-element.794) | copy-start | bytes 18436
  672.9 132.9 %reduce-scatter.12.cloned.1.call-start = ((), (), s32[]{:S(2)}) async-start(), calls=%async_computation.17 | async-start | bytes 8601600 | tf_op jit(solution)/shard_map/reduce_scatter | solution.py:83
  743.3 78.5 %copy-start.8 = (bf16[1536,280]{0,1:T(8,128)(2,1)S(1)}, bf16[1536,280]{0,1:T(8,128)(2,1)}, u32[]{:S(2)}) copy-start(bf16[1536,280]{0,1:T(8,128)(2,1)} %copy.122) | copy-start | bytes 2580484
  743.3 78.5 %copy-start.27 = (pred[1536]{0:T(1024)(128)(4,1)S(1)}, pred[1536]{0:T(1024)(128)(4,1)}, u32[]{:S(2)}) copy-start(pred[1536]{0:T(1024)(128)(4,1)} %copy-done.25) | copy-start | bytes 4612
  743.3 78.5 %copy-start.31 = (pred[1536]{0:T(1024)(128)(4,1)S(1)}, pred[1536]{0:T(1024)(128)(4,1)}, u32[]{:S(2)}) copy-start(pred[1536]{0:T(1024)(128)(4,1)} %copy-done.29) | copy-start | bytes 4612
  743.3 113.4 %all-gather.17.cloned.1.call-start = ((), (), s32[]{:S(2)}) async-start(), calls=%async_computation.18 | async-start | bytes 4300800 | tf_op jit(solution)/shard_map/all_gather | solution.py:79
  825.4 313.7 %reduce-scatter.14.cloned.1.call-start = ((), (), s32[]{:S(2)}) async-start(), calls=%async_computation.19 | async-start | bytes 8601600 | tf_op jit(solution)/shard_map/reduce_scatter | solution.py:83
  1076.5 594.8 %all-reduce.10.cloned.1.call-start = ((), (), s32[]{:S(2)}) async-start(), calls=%async_computation.20 | async-start | bytes 30965760 | tf_op jit(solution)/shard_map/psum | solution.py:414
  1110.9 28.1 %copy-start.34 = (f32[1536]{0:T(1024)S(1)}, f32[1536]{0:T(1024)}, u32[]{:S(2)}) copy-start(f32[1536]{0:T(1024)} %copy-done.33) | copy-start | bytes 18436
  1110.9 28.1 %copy-start.36 = (f32[1536]{0:T(1024)S(1)}, f32[1536]{0:T(1024)}, u32[]{:S(2)}) copy-start(f32[1536]{0:T(1024)} %copy-done.35) | copy-start | bytes 18436
  1110.9 28.1 %copy-start.48 = (f32[280]{0:T(512)S(1)}, f32[280]{0:T(512)}, u32[]{:S(2)}) copy-start(f32[280]{0:T(512)} %param.29) | copy-start | bytes 3364
  1214.5 461.1 %all-to-all-start.3 = ((bf16[8,500,280]{1,2,0:T(8,128)(2,1)}), bf16[8,500,280]{1,2,0:T(8,128)(2,1)}, u32[]{:S(2)}, u32[]{:S(2)}) async-start(bf16[8,500,280]{1,2,0:T(8,128)(2,1)} %copy.130), calls=%async_computation.8 | async-start | bytes 4587520 | tf_op jit(solution)/shard_map/all_to_all | solution.py:398
  1675.6 57.3 %all-to-all-start.1 = ((bf16[8,500,280]{1,2,0:T(8,128)(2,1)}), bf16[8,500,280]{1,2,0:T(8,128)(2,1)}, u32[]{:S(2)}, u32[]{:S(2)}) async-start(bf16[8,500,280]{1,2,0:T(8,128)(2,1)} %copy.114), calls=%async_computation.3 | async-start | bytes 4587520 | tf_op jit(solution)/shard_map/all_to_all | solution.py:397
  (56 other events, 504.4 us)
Sparse Core Ops, SparseCore 0:
  179.3 29.4 all-gather.6
  276.1 62.2 reduce-scatter.5
  372.7 28.5 all-gather.8
  422.2 62.3 reduce-scatter.7
  501.9 31.2 all-gather.10
  594.1 62.2 reduce-scatter.9
  658.7 30.2 all-gather.12
  691.2 30.1 all-gather.14
  743.4 62.2 reduce-scatter.11
  825.5 31.2 all-gather.16
  1076.6 62.3 reduce-scatter.13
  1145.5 525.7 all-reduce.9
where the time goes:
time: 1790 us; the launch traced here: 1780 us
  waiting for transfers between devices  799 us (45%)
  matrix products  327 us (18%)
  local copies, waits for them, and re-layouts  299 us (17%)
  blocking collectives  206 us (12%)
  other arithmetic  97.7 us (5%)
  starting transfers between devices  19.2 us (1%)
    psum x1, waiting for transfers between devices, shards(): lax.psum((grads[0], grads[1], grads[2], grads[3], grads[4], grads[5], gra...  358 us
    reduce_scatter x3, waiting for transfers between devices, sum_branch(): lax.psum_scatter(partial_value, 'tensor', scatter_dimension=1, tiled=True)  124 us
    all_gather x4, waiting for transfers between devices, gather_normed(): return lax.all_gather(values, 'tensor', axis=1, tiled=True)  111 us
    psum x1, blocking collectives, shards(): lax.psum((grads[0], grads[1], grads[2], grads[3], grads[4], grads[5], gra...  84.8 us
    reduce_scatter x2, waiting for transfers between devices, sum_input_grad(): lax.psum_scatter(partial_value, 'tensor', scatter_dimension=1, tiled=True)  72.1 us
    all_to_all x1, blocking collectives, shards(): lax.all_to_all(sent_grads, 'dp', split_axis=0, concat_axis=0, tiled=True)  58.3 us
    dot_general x2, matrix products, one_block(): jnp.einsum('hqk,qhd->khd', grad_scores, query_block, preferred_element_ty...  54.4 us
    dot_general x2, matrix products, one_block(): jnp.einsum('hqk,khd->qhd', grad_scores, key_block, preferred_element_type...  52.8 us
  transfers between devices with their start and end apart: 15, of which 13 were waited for; matrix products, arithmetic and copies ran while one was open for 10% of the time, Pallas kernels for 0%

commit v1 on v0

v1 whole, which is shorter than its diff:
```python
import functools

import jax
import jax.numpy as jnp
from jax import lax
from jax.experimental import pallas as pl
from jax.experimental.pallas import tpu as pltpu
from jax.sharding import PartitionSpec as P

D = 1120
HD = 56
EPS = 1e-05
BF = jnp.bfloat16
F32 = jnp.float32
QB = 256
TAIL = 512
SCALE = HD ** (-0.5)


def swap(value, axis, mask):
    size = lax.axis_size(axis)
    return lax.ppermute(value, axis, [(i, i ^ mask) for i in range(size)])


def dot(left, right, dims=((1,), (0,))):
    return lax.dot_general(left, right, (dims, ((), ())), preferred_element_type=F32)


def gelu_tanh(values):
    return jax.nn.gelu(values, approximate=True)


def vmem_whole(shape):
    return pl.BlockSpec(shape, lambda i, *_: (0,) * len(shape))


def assemble_kernel(place, own, near, far, cross, out):
    parts = (own, near, far, cross)
    for mine in range(4):

        @pl.when(place[0] == mine)
        def _(mine=mine):
            out[...] = jnp.concatenate([parts[j ^ mine][...] for j in range(4)], axis=1)


def norm_kernel(place, own, near, far, cross, gain, bias, out, normed):
    assemble_kernel(place, own, near, far, cross, out)
    values = out[...].astype(F32)
    mean_row = jnp.sum(values, axis=1, keepdims=True) * (1.0 / D)
    centered = values - mean_row
    var_row = jnp.sum(centered * centered, axis=1, keepdims=True) * (1.0 / D)
    normed[...] = (centered * lax.rsqrt(var_row + EPS) * gain[...] + bias[...]).astype(BF)


def gather_columns(value):
    near = swap(value, "tensor", 1)
    far = swap(value, "tensor", 2)
    cross = swap(far, "tensor", 1)
    return (value, near, far, cross)


def assemble(parts, place, row_map=None, affine=None):
    rows = parts[0].shape[0]
    step = 256
    spec_in = pl.BlockSpec((step, 280), (lambda i, p: (i, 0)) if row_map is None else row_map)
    spec_out = pl.BlockSpec((step, D), lambda i, p: (i, 0))
    full = jax.ShapeDtypeStruct((rows, D), BF)
    if affine is None:
        body, extra, outs, specs = assemble_kernel, (), full, spec_out
        extra_specs = []
    else:
        body, extra, outs, specs = norm_kernel, affine, (full, full), (spec_out, spec_out)
        extra_specs = [vmem_whole((1, D))] * 2
    return pl.pallas_call(
        body,
        out_shape=outs,
        grid_spec=pltpu.PrefetchScalarGridSpec(
            num_scalar_prefetch=1,
            grid=(rows // step,),
            in_specs=[spec_in] * 4 + extra_specs,
            out_specs=specs,
        ),
        compiler_params=pltpu.CompilerParams(
            dimension_semantics=("arbitrary",), vmem_limit_bytes=16 << 20
        ),
        cost_estimate=pl.CostEstimate(
            flops=rows * D * 10, bytes_accessed=rows * D * 6, transcendentals=0
        ),
    )(place, *parts, *extra)


def first_of(rows, bounds):
    start = jnp.zeros_like(rows)
    for bound in bounds:
        start = jnp.where(rows >= bound, bound, start)
    return start


def block_setup(bounds, step):
    base = step * QB
    low = first_of(base, bounds)
    count = step - low // QB + 1
    return (base, count)


def allowed_keys(bounds, base, width):
    shape = (width, QB)
    keys = base + QB - width + lax.broadcasted_iota(jnp.int32, shape, 0)
    rows = base + lax.broadcasted_iota(jnp.int32, (1, QB), 1)
    return (keys >= first_of(rows, bounds)) & (keys <= rows)


def attend_kernel(heads, table, qkv, mixed, lse, kbuf, vtbuf):
    step = pl.program_id(0)
    cols = heads * HD
    bounds = [table[k] for k in range(4)]
    base, count = block_setup(bounds, step)

    @pl.when(step == 0)
    def _():
        for h in range(heads):
            kbuf[h] = qkv[:, cols + HD * h : cols + HD * (h + 1)]
            vtbuf[h] = qkv[:, 2 * cols + HD * h : 2 * cols + HD * (h + 1)].T

    @pl.when(base >= bounds[3])
    def _():
        mixed[...] = jnp.zeros_like(mixed)
        lse[...] = jnp.zeros_like(lse)

    for blocks in range(1, 4):

        @pl.when((count == blocks) & (base < bounds[3]))
        def _(blocks=blocks):
            width = blocks * QB
            offset = pl.multiple_of(base + QB - width, QB)
            allowed = allowed_keys(bounds, base, width)
            query = qkv[pl.ds(pl.multiple_of(base, QB), QB), :cols]
            pieces = []
            for h in range(heads):
                keys = kbuf[h, pl.ds(offset, width), :]
                scores = dot(keys, query[:, HD * h : HD * (h + 1)], ((1,), (1,))) * SCALE
                scores = jnp.where(allowed, scores, -1e30)
                top = jnp.max(scores, axis=0, keepdims=True)
                shifted = jnp.exp(scores - top)
                total = jnp.sum(shifted, axis=0, keepdims=True)
                weights = (shifted * (1.0 / total)).astype(BF)
                pieces.append(dot(vtbuf[h, :, pl.ds(offset, width)], weights))
                lse[h : h + 1, :] = top + jnp.log(total)
            mixed[...] = jnp.concatenate(pieces, axis=0).T.astype(BF)


def attend(table, qkv):
    rows, cols = qkv.shape[0], qkv.shape[1] // 3
    heads = cols // HD
    return pl.pallas_call(
        functools.partial(attend_kernel, heads),
        out_shape=(
            jax.ShapeDtypeStruct((rows, cols), BF),
            jax.ShapeDtypeStruct((8, rows), F32),
        ),
        grid_spec=pltpu.PrefetchScalarGridSpec(
            num_scalar_prefetch=1,
            grid=(rows // QB,),
            in_specs=[vmem_whole((rows, 3 * cols))],
            out_specs=(
                pl.BlockSpec((QB, cols), lambda i, *_: (i, 0)),
                pl.BlockSpec((8, QB), lambda i, *_: (0, i)),
            ),
            scratch_shapes=[
                pltpu.VMEM((heads, rows, HD), BF),
                pltpu.VMEM((heads, HD, rows), BF),
            ],
        ),
        compiler_params=pltpu.CompilerParams(
            dimension_semantics=("arbitrary",), vmem_limit_bytes=32 << 20
        ),
        cost_estimate=pl.CostEstimate(
            flops=4 * rows * 512 * 256 * heads,
            bytes_accessed=rows * cols * 8,
            transcendentals=rows * 512 * heads,
        ),
    )(table, qkv)


def attend_back_kernel(
    heads, table, qkv, lse, gmix, out, kbuf, vbuf, ktbuf, dkbuf, dvbuf, dqbuf
):
    step = pl.program_id(0)
    cols = heads * HD
    bounds = [table[k] for k in range(4)]
    base, count = block_setup(bounds, step)
    here = pl.ds(pl.multiple_of(base, QB), QB)

    @pl.when(step == 0)
    def _():
        for h in range(heads):
            keys = qkv[:, cols + HD * h : cols + HD * (h + 1)]
            kbuf[h] = keys
            ktbuf[h] = keys.T
            vbuf[h] = qkv[:, 2 * cols + HD * h : 2 * cols + HD * (h + 1)]
        dkbuf[...] = jnp.zeros_like(dkbuf)
        dvbuf[...] = jnp.zeros_like(dvbuf)

    @pl.when(base >= bounds[3])
    def _():
        dqbuf[here, :] = jnp.zeros((QB, cols), BF)

    for blocks in range(1, 4):

        @pl.when((count == blocks) & (base < bounds[3]))
        def _(blocks=blocks):
            width = blocks * QB
            window = pl.ds(pl.multiple_of(base + QB - width, QB), width)
            allowed = allowed_keys(bounds, base, width)
            query = qkv[here, :cols]
            grads = gmix[...]
            pieces = []
            for h in range(heads):
                one_query = query[:, HD * h : HD * (h + 1)]
                one_grad = grads[:, HD * h : HD * (h + 1)]
                scores = dot(kbuf[h, window, :], one_query, ((1,), (1,))) * SCALE
                probs = jnp.exp(jnp.where(allowed, scores, -1e30) - lse[h : h + 1, :])
                grad_probs = dot(vbuf[h, window, :], one_grad, ((1,), (1,)))
                dvbuf[h, window, :] += dot(probs.astype(BF), one_grad)
                delta = jnp.sum(probs * grad_probs, axis=0, keepdims=True)
                grad_scores = (probs * (grad_probs - delta) * SCALE).astype(BF)
                dkbuf[h, window, :] += dot(grad_scores, one_query)
                pieces.append(dot(ktbuf[h, :, window], grad_scores))
            dqbuf[here, :] = jnp.concatenate(pieces, axis=0).T.astype(BF)

    @pl.when(step == pl.num_programs(0) - 1)
    def _():
        out[:, :cols] = dqbuf[...]
        out[:, cols : 2 * cols] = jnp.concatenate(
            [dkbuf[h].astype(BF) for h in range(heads)], axis=1
        )
        out[:, 2 * cols :] = jnp.concatenate([dvbuf[h].astype(BF) for h in range(heads)], axis=1)


def attend_back(table, qkv, lse, gmix):
    rows, cols = qkv.shape[0], qkv.shape[1] // 3
    heads = cols // HD
    return pl.pallas_call(
        functools.partial(attend_back_kernel, heads),
        out_shape=jax.ShapeDtypeStruct((rows, 3 * cols), BF),
        grid_spec=pltpu.PrefetchScalarGridSpec(
            num_scalar_prefetch=1,
            grid=(rows // QB,),
            in_specs=[
                vmem_whole((rows, 3 * cols)),
                pl.BlockSpec((8, QB), lambda i, *_: (0, i)),
                pl.BlockSpec((QB, cols), lambda i, *_: (i, 0)),
            ],
            out_specs=vmem_whole((rows, 3 * cols)),
            scratch_shapes=[
                pltpu.VMEM((heads, rows, HD), BF),
                pltpu.VMEM((heads, rows, HD), BF),
                pltpu.VMEM((heads, HD, rows), BF),
                pltpu.VMEM((heads, rows, HD), F32),
                pltpu.VMEM((heads, rows, HD), F32),
                pltpu.VMEM((rows, cols), BF),
            ],
        ),
        compiler_params=pltpu.CompilerParams(
            dimension_semantics=("arbitrary",), vmem_limit_bytes=48 << 20
        ),
        cost_estimate=pl.CostEstimate(
            flops=10 * rows * 512 * 256 * heads,
            bytes_accessed=rows * cols * 16,
            transcendentals=rows * 512 * heads,
        ),
    )(table, qkv, lse, gmix)


def row_block(value, index, count):
    return lax.dynamic_slice_in_dim(value, index * count, count)


def col_block(value, index, count):
    return lax.dynamic_slice_in_dim(value, index * count, count, axis=1)


def fold_rows(keep, send):
    got = swap(send, "tensor", 1)
    both = keep + got.astype(F32)
    half = both.shape[0] // 2
    last = swap(both[half:].astype(BF), "tensor", 2)
    return both[:half] + last.astype(F32)


def fold_cols(keep, send, own_order=False):
    got = swap(send, "tensor", 1)
    if own_order:
        got = reorder(got, (2, 3, 0, 1))
    both = keep + got.astype(F32)
    half = both.shape[1] // 2
    last = swap(both[:, half:].astype(BF), "tensor", 2)
    if own_order:
        last = reorder(last, (1, 0, 3, 2))
    return both[:, :half] + last.astype(F32)


def reorder(value, blocks):
    count = value.shape[0] // len(blocks)
    return jnp.concatenate([value[b * count : (b + 1) * count] for b in blocks])


def spread_rows(value):
    near = swap(value, "tensor", 1)
    far = swap(value, "tensor", 2)
    cross = swap(far, "tensor", 1)
    return jnp.concatenate([value, far, near, cross], axis=0)


def total_over(value, axis):
    mask = 1
    while mask < lax.axis_size(axis):
        value = value + swap(value, axis, mask)
        mask *= 2
    return value


def shards(
    x_home,
    cot_home,
    cell_len,
    norm1_gain,
    norm1_bias,
    qkv_weight,
    out_weight,
    norm2_gain,
    norm2_bias,
    up_weight,
    down_weight,
):
    groups = cell_len.shape[0]
    home_rows, cols = x_home.shape
    rows = -(-home_rows // 512) * 512
    block = rows // 4
    me = lax.axis_index("tensor")
    group = lax.axis_index("dp")
    order = (me, me ^ 2, me ^ 1, me ^ 3)
    weight = groups / jnp.sum(cell_len).astype(F32)
    my_len = lax.dynamic_index_in_dim(cell_len, group, 0, keepdims=False)
    table = jnp.cumsum(my_len).astype(jnp.int32)
    live_count = table[3]
    place = me.reshape(1).astype(jnp.int32)

    pad = ((0, rows - home_rows), (0, 0))
    live = (jnp.arange(rows) < live_count)[:, None]
    x_own = jnp.pad(x_home, pad)
    cot_own = jnp.where(live, jnp.pad(cot_home, pad), jnp.zeros((), BF))

    affine = jnp.stack([norm1_gain, norm1_bias, norm2_gain, norm2_bias])
    affine_parts = gather_columns(affine)
    affine_all = jnp.stack(affine_parts)
    gain_one, bias_one, gain_two, bias_two = (
        jnp.concatenate(
            [lax.dynamic_index_in_dim(affine_all, me ^ j, 0, keepdims=False)[k] for j in range(4)]
        )[None, :]
        for k in range(4)
    )

    w_qkv = qkv_weight.reshape(D, 3 * cols)

    x_parts = gather_columns(x_own)
    x_full, full_one = assemble(x_parts, place, affine=(gain_one, bias_one))
    cot_parts = gather_columns(cot_own)
    qkv = dot(full_one, w_qkv).astype(BF)
    mixed, lse = attend(table, qkv)
    mixed_rel = jnp.concatenate([row_block(mixed, j, block) for j in order])
    half = rows // 2
    middle = row_block(x_full, me, block).astype(F32) + fold_rows(
        dot(mixed_rel[:half], out_weight), dot(mixed_rel[half:], out_weight).astype(BF)
    )
    mean_two = jnp.mean(middle, axis=1, keepdims=True)
    inv_two = lax.rsqrt(jnp.mean(jnp.square(middle - mean_two), axis=1, keepdims=True) + EPS)
    hat_two = (middle - mean_two) * inv_two
    full_two = spread_rows((hat_two * gain_two + bias_two).astype(BF))

    steps = block // 256

    def row_map(i, p):
        rel = i // steps
        mask = (rel % 2) * 2 + rel // 2
        return ((p[0] ^ mask) * steps + i % steps, 0)

    g_full = assemble(cot_parts, place, row_map=row_map)
    hidden_pre = dot(full_two, up_weight)
    hidden_f32, gelu_pull = jax.vjp(gelu_tanh, hidden_pre)
    hidden = hidden_f32.astype(BF)
    grad_pre = gelu_pull(dot(g_full, down_weight, ((1,), (1,))))[0].astype(BF)
    grad_norm_two = fold_rows(
        dot(grad_pre[:half], up_weight, ((1,), (1,))),
        dot(grad_pre[half:], up_weight, ((1,), (1,))).astype(BF),
    )
    grad_up = dot(full_two, grad_pre, ((0,), (0,))).astype(BF)
    grad_down = dot(hidden, g_full, ((0,), (0,))).astype(BF)
    grad_up, grad_down = lax.psum((grad_up, grad_down), "dp")

    down_rel = [col_block(down_weight, j, cols) for j in order]
    down_keep = jnp.concatenate(down_rel[:2], axis=1)
    down_send = jnp.concatenate(down_rel[2:], axis=1)
    middle_rel = [col_block(middle, j, cols) for j in order]
    skip = ((0, rows - block), (0, 0))
    out_rel = fold_cols(
        dot(hidden, down_keep) + jnp.pad(jnp.concatenate(middle_rel[:2], axis=1), skip),
        (dot(hidden, down_send) + jnp.pad(jnp.concatenate(middle_rel[2:], axis=1), skip)).astype(BF),
        own_order=True,
    ).astype(BF)

    def natural_rows(value):
        where = (0, 2, 1, 3)
        slot = [me ^ j for j in range(4)]
        spot = jnp.array(where, jnp.int32)
        return jnp.concatenate([row_block(value, spot[s], block) for s in slot])

    out_rows = jnp.where(live, natural_rows(out_rel), jnp.zeros((), BF))[:home_rows]

    a_two = grad_norm_two * gain_two
    grad_middle = row_block(g_full, 0, block).astype(F32) + inv_two * (
        a_two
        - jnp.mean(a_two, axis=1, keepdims=True)
        - hat_two * jnp.mean(a_two * hat_two, axis=1, keepdims=True)
    )
    gm_full = spread_rows(grad_middle.astype(BF))
    grad_out_w = dot(mixed_rel, gm_full, ((0,), (0,))).astype(BF)
    grad_mixed = natural_rows(dot(gm_full, out_weight, ((1,), (1,))).astype(BF))
    grad_joined = attend_back(table, qkv, lse, grad_mixed)
    grad_qkv = dot(full_one, grad_joined, ((0,), (0,))).astype(BF)
    grad_qkv, grad_out_w = lax.psum((grad_qkv, grad_out_w), "dp")

    w_rel = [row_block(w_qkv, j, cols) for j in order]
    grad_norm_one = fold_cols(
        dot(grad_joined, jnp.concatenate(w_rel[:2]), ((1,), (1,))),
        dot(grad_joined, jnp.concatenate(w_rel[2:]), ((1,), (1,))).astype(BF),
    )
    x_wide = x_full.astype(F32)
    mean_one = jnp.mean(x_wide, axis=1, keepdims=True)
    inv_one = lax.rsqrt(jnp.mean(jnp.square(x_wide - mean_one), axis=1, keepdims=True) + EPS)
    hat_one = (x_own.astype(F32) - mean_one) * inv_one
    a_one = grad_norm_one * norm1_gain
    sums = total_over(jnp.stack([jnp.sum(a_one, axis=1), jnp.sum(a_one * hat_one, axis=1)]), "tensor")
    gm_own = natural_rows(
        lax.switch(me, [lambda v, j=j: v[:, cols * j : cols * (j + 1)] for j in range(4)], gm_full)
    )
    x_grad = gm_own.astype(F32) + inv_one * (
        a_one - sums[0][:, None] / D - hat_one * (sums[1][:, None] / D)
    )
    x_grad = x_grad.astype(BF)[:home_rows]

    two = jnp.stack([jnp.sum(grad_norm_two * hat_two, axis=0), jnp.sum(grad_norm_two, axis=0)])
    two = total_over(two, "tensor")
    two = lax.dynamic_slice_in_dim(two, me * cols, cols, axis=1)
    one = jnp.stack([jnp.sum(grad_norm_one * hat_one, axis=0), jnp.sum(grad_norm_one, axis=0)])
    small = total_over(jnp.concatenate([one, two]), "dp") * weight

    def scaled(item):
        return item.astype(F32) * weight

    return (
        out_rows,
        x_grad,
        small[0],
        small[1],
        scaled(grad_qkv).reshape(D, 3, cols),
        scaled(grad_out_w),
        small[2],
        small[3],
        scaled(grad_up),
        scaled(grad_down),
    )


def solution(mesh):
    rows, vector = P("dp", "tensor"), P("tensor")
    qkv, wide, tall = P(None, None, "tensor"), P(None, "tensor"), P("tensor", None)
    return jax.shard_map(
        shards,
        mesh=mesh,
        in_specs=(rows, rows, P(), vector, vector, qkv, tall, vector, vector, wide, tall),
        out_specs=(rows, rows, vector, vector, qkv, tall, vector, vector, wide, tall),
        check_vma=False,
    )
```

time: 1790 us -> 736 us (0.41)
  waiting for transfers between devices: 799 us -> 300 us
  matrix products: 327 us -> 114 us
  blocking collectives: 206 us -> 0 us
  local copies, waits for them, and re-layouts: 299 us -> 141 us
  Pallas kernels: 0 us -> 70.4 us
  other arithmetic: 97.7 us -> 70.9 us
    dot_general x30 -> x16, matrix products: 311 us -> 114 us  [dot(): lax.dot_general(left, right, (dims, ((), ())), preferred_element_type=F32)]
    reduce_scatter x5 -> x0, waiting for transfers between devices: 196 us -> none  [the longest x3 124 us: sum_branch(): lax.psum_scatter(partial_value, 'tensor', scatter_dimension=1, tiled=True)]
    psum x1, waiting for transfers between devices: 358 us -> 163 us  [shards(): grad_qkv, grad_out_w = lax.psum((grad_qkv, grad_out_w), 'dp')]
    all_gather x6 -> x0, waiting for transfers between devices: 158 us -> none  [the longest x4 111 us: gather_normed(): return lax.all_gather(values, 'tensor', axis=1, tiled=True)]
    psum x7 -> x0, blocking collectives: 147 us -> none  [the longest x1 84.8 us: shards(): lax.psum((grads[0], grads[1], grads[2], grads[3], grads[4], grads[5], gra...]
    ppermute x0 -> x30, waiting for transfers between devices: none -> 137 us  [swap(): return lax.ppermute(value, axis, [(i, i ^ mask) for i in range(size)])]
    gather x14 -> x0, local copies, waits for them, and re-layouts: 116 us -> none  [the longest x1 18.3 us: shards(): jnp.take(cot_home, send_pick, axis=0).reshape(groups, MAXLEN, col_count)]
    all_to_all x3 -> x0, waiting for transfers between devices: 85.2 us -> none  [the longest x1 52 us: shards(): lax.all_to_all(sent_rows, 'dp', split_axis=0, concat_axis=0, tiled=True)]
  transfers between devices with their start and end apart: 15 -> 31, of which waited for: 13 -> 15; matrix products, arithmetic and copies ran while one was open for 10% -> 26% of each run, Pallas kernels for 0% -> 0%
where the time goes in v1:
time: 736 us; the launch traced here: 733 us
  waiting for transfers between devices  300 us (41%)
  local copies, waits for them, and re-layouts  141 us (19%)
  matrix products  114 us (15%)
  other arithmetic  70.9 us (10%)
  Pallas kernels  70.4 us (10%)
  starting transfers between devices  18.8 us (3%)
  between operations  18.7 us (3%)
    psum x1, waiting for transfers between devices, shards(): grad_qkv, grad_out_w = lax.psum((grad_qkv, grad_out_w), 'dp')  163 us
    ppermute x30, waiting for transfers between devices, swap(): return lax.ppermute(value, axis, [(i, i ^ mask) for i in range(size)])  137 us
    dot_general x16, matrix products, dot(): lax.dot_general(left, right, (dims, ((), ())), preferred_element_type=F32)  114 us
    unnamed x156, local copies, waits for them, and re-layouts  47.1 us
    ppermute x15, local copies, waits for them, and re-layouts, swap(): return lax.ppermute(value, axis, [(i, i ^ mask) for i in range(size)])  36.3 us
    pallas_call x1, Pallas kernels, attend_back(): pl.pallas_call(functools.partial(attend_back_kernel, heads), out_shape=ja...  35.2 us
    pallas_call x1, Pallas kernels, attend(): pl.pallas_call(functools.partial(attend_kernel, heads), out_shape=(jax.Sh...  27.7 us
    ppermute x30, starting transfers between devices, swap(): return lax.ppermute(value, axis, [(i, i ^ mask) for i in range(size)])  18.7 us
  transfers between devices with their start and end apart: 31, of which 15 were waited for; matrix products, arithmetic and copies ran while one was open for 26% of the time, Pallas kernels for 0%

profile of v1, /device:TPU:0, one launch (start us, length us, event | category | flops | bytes accessed | tf_op | source)
XLA Modules:
  0.0 733.0 jit_solution(11610046471144164109)
XLA Ops:
  18.1 25.6 %collective-permute-done.1 = bf16[2048,280]{0,1:T(8,128)(2,1)} collective-permute-done((bf16[2048,280]{0,1:T(8,128)(2,1)}, bf16[2048,280]{0,1:T(8,128)(2,1)}, u32[]{:S(2)}, u32[]{:S(2)}) %collective-permute-start.1) | collective-permute-done | bytes 1146912 | tf_op jit(solution)/shard_map/ppermute | solution.py:22
  62.2 5.4 shard_map.213
  69.8 5.7 convolution_convert_fusion.4.qkv
  75.5 27.7 %shard_map.214 = (bf16[2048,280]{1,0:T(8,128)(2,1)S(1)}, f32[8,2048]{1,0:T(8,128)S(1)}) custom-call(s32[4]{0:T(128)S(1)} %bitcast.45, bf16[2048,840]{1,0:T(8,128)(2,1)S(1)} %convolution_convert_fusion.4.qkv), custom_call_target="tpu_custom_call" | custom-call | flops 5368709120 | bytes 4587520 | tf_op jit(solution)/shard_map/pallas_call | solution.py:155
  110.4 5.0 copy.94
  137.0 16.8 %collective-permute-done.7 = bf16[512,1120]{0,1:T(8,128)(2,1)} collective-permute-done((bf16[512,1120]{0,1:T(8,128)(2,1)}, bf16[512,1120]{0,1:T(8,128)(2,1)}, u32[]{:S(2)}, u32[]{:S(2)}) %collective-permute-start.7) | collective-permute-done | bytes 1146912 | tf_op jit(solution)/shard_map/ppermute | solution.py:22
  165.9 12.5 %collective-permute-done.14 = bf16[2048,280]{0,1:T(8,128)(2,1)} collective-permute-done((bf16[2048,280]{0,1:T(8,128)(2,1)}, bf16[2048,280]{0,1:T(8,128)(2,1)}, u32[]{:S(2)}, u32[]{:S(2)}) %collective-permute-start.14) | collective-permute-done | bytes 1146912 | tf_op jit(solution)/shard_map/ppermute | solution.py:22
  178.8 23.3 %collective-permute-done.8 = bf16[512,1120]{0,1:T(8,128)(2,1)} collective-permute-done((bf16[512,1120]{0,1:T(8,128)(2,1)}, bf16[512,1120]{0,1:T(8,128)(2,1)}, u32[]{:S(2)}, u32[]{:S(2)}) %collective-permute-start.8) | collective-permute-done | bytes 1146912 | tf_op jit(solution)/shard_map/ppermute | solution.py:22
  205.4 4.9 constant_dynamic-slice_fusion.20
  238.9 12.2 %fusion.47 = f32[2048,1120]{0,1:T(8,128)} fusion(bf16[1120,1120]{1,0:T(8,128)(2,1)S(1)} %copy-done, bf16[512,1120]{1,0:T(8,128)(2,1)} %copy.101, bf16[512,1120]{1,0:T(8,128)(2,1)} %copy.100, bf16[512,1120]{1,0:T(8,128)(2,1)} %copy.99, bf16[512,1120]{1,0:T(8,128)(2,1)} %add_convert_fusion.1), kind=kOutput, calls=%fused_computation.97 | convolution fusion | flops 5156372480 | bytes 16271360 | tf_op jit(solution)/shard_map/dot_general | solution.py:26
  251.1 12.8 %fusion.8 = bf16[2048,1120]{0,1:T(8,128)(2,1)S(1)} fusion(f32[2048,1120]{0,1:T(8,128)} %fusion.47, bf16[2048,1120]{1,0:T(8,128)(2,1)S(1)} %bitcast.42, bf16[1120,1120]{1,0:T(8,128)(2,1)S(1)} %copy-done.30), kind=kOutput, calls=%fused_computation.12 | convolution fusion | flops 5183897600 | bytes 20858880 | tf_op jit(solution)/shard_map/dot_general | solution.py:26
  264.0 4.5 convolution_convert_fusion.3
  271.9 8.4 %fusion.10 = bf16[2048,560]{1,0:T(8,128)(2,1)} fusion(f32[512,280]{1,0:T(8,128)S(1)} %get-tuple-element.99, f32[512,280]{1,0:T(8,128)S(1)} %get-tuple-element.98, bf16[1120,280]{1,0:T(8,128)(2,1)S(1)} %copy-done.45, bf16[1120,280]{1,0:T(8,128)(2,1)S(1)} %copy-done.44, f32[2048,1120]{0,1:T(8,128)S(1)} %copy-done.66), kind=kOutput, calls=%fused_computation.18 | convolution fusion | flops 2599045120 | bytes 13870080 | tf_op jit(solution)/shard_map/dot_general | solution.py:26
  280.3 4.4 copy.104
  285.1 7.4 %fusion.20 = f32[1024,1120]{1,0:T(8,128)} fusion(bf16[1120,1120]{1,0:T(8,128)(2,1)S(1)} %copy-done, bf16[2048,1120]{0,1:T(8,128)(2,1)} %copy-done.65), kind=kOutput, calls=%fused_computation.60 | convolution fusion | flops 2569011200 | bytes 9390080 | tf_op jit(solution)/shard_map/dot_general | solution.py:26
  292.5 4.5 copy.119
  306.7 12.8 %convolution_convert_fusion = bf16[1120,1120]{1,0:T(8,128)(2,1)} fusion(bf16[2048,1120]{1,0:T(8,128)(2,1)} %copy-done.5, f32[2048,1120]{0,1:T(8,128)} %fusion.47), kind=kOutput, calls=%fused_computation.14 | convolution fusion | flops 5159920640 | bytes 16271360 | tf_op jit(solution)/shard_map/dot_general | solution.py:26
  328.1 4.5 collective-permute-done.17
  345.8 11.8 %fusion.12 = f32[2048,560]{1,0:T(8,128)S(1)} fusion(f32[512,280]{1,0:T(8,128)} %get-tuple-element.100, f32[512,280]{1,0:T(8,128)} %get-tuple-element.101, bf16[1024,560]{1,0:T(8,128)(2,1)} %copy.142, bf16[1024,560]{1,0:T(8,128)(2,1)} %copy.141, bf16[1120,280]{1,0:T(8,128)(2,1)} %get-tuple-element.96, bf16[1120,280]{1,0:T(8,128)(2,1)} %get-tuple-element.94, ...), kind=kOutput, calls=%fused_computation.21 | convolution fusion | flops 2603632640 | bytes 18457600 | tf_op jit(solution)/shard_map/dot_general | solution.py:26
  362.5 10.1 %collective-permute-done.18 = bf16[512,1120]{0,1:T(8,128)(2,1)} collective-permute-done((bf16[512,1120]{0,1:T(8,128)(2,1)}, bf16[512,1120]{0,1:T(8,128)(2,1)}, u32[]{:S(2)}, u32[]{:S(2)}) %collective-permute-start.18) | collective-permute-done | bytes 1146912 | tf_op jit(solution)/shard_map/ppermute | solution.py:22
  372.6 11.5 %convolution_convert_fusion.1 = bf16[1120,1120]{1,0:T(8,128)(2,1)} fusion(bf16[2048,1120]{0,1:T(8,128)(2,1)} %copy-done.65, bf16[512,1120]{1,0:T(8,128)(2,1)} %copy.101, bf16[512,1120]{1,0:T(8,128)(2,1)} %copy.100, bf16[512,1120]{1,0:T(8,128)(2,1)} %copy.99, bf16[512,1120]{1,0:T(8,128)(2,1)} %add_convert_fusion.1), kind=kOutput, calls=%fused_computation.15 | convolution fusion | flops 5157626880 | bytes 11683840 | tf_op jit(solution)/shard_map/dot_general | solution.py:26
  384.2 11.1 %collective-permute-done.12 = bf16[2048,280]{0,1:T(8,128)(2,1)S(1)} collective-permute-done((bf16[2048,280]{0,1:T(8,128)(2,1)}, bf16[2048,280]{0,1:T(8,128)(2,1)S(1)}, u32[]{:S(2)}, u32[]{:S(2)}) %collective-permute-start.12) | collective-permute-done | bytes 1146912 | tf_op jit(solution)/shard_map/ppermute | solution.py:22
  414.5 35.2 %shard_map.216 = bf16[2048,840]{1,0:T(8,128)(2,1)S(1)} custom-call(s32[4]{0:T(128)S(1)} %bitcast.46, bf16[2048,840]{1,0:T(8,128)(2,1)} %copy-done.17, f32[8,2048]{1,0:T(8,128)S(1)} %get-tuple-element.26.lse, bf16[2048,280]{1,0:T(8,128)(2,1)S(1)} %pad_maximum_fusion.2.gmix), custom_call_target="tpu_custom_call" | custom-call | flops 13421772800 | bytes 9175040 | tf_op jit(solution)/shard_map/pallas_call | solution.py:243
  449.7 6.2 convolution_convert_fusion.5
  469.3 6.4 fusion.39
  479.2 4.6 add.267
  494.3 21.8 %collective-permute-done.26 = f32[2,1120]{1,0:T(2,128)S(1)} collective-permute-done((f32[2,1120]{1,0:T(2,128)S(1)}, f32[2,1120]{1,0:T(2,128)S(1)}, u32[]{:S(2)}, u32[]{:S(2)}) %collective-permute-start.26) | collective-permute-done | bytes 8992 | tf_op jit(solution)/shard_map/ppermute | solution.py:22
  518.7 5.4 fusion.87
  524.4 4.9 fusion.29
  534.1 5.1 collective-permute-done.29
  543.1 7.3 %fusion.17 = bf16[2000,280]{1,0:T(8,128)(2,1)S(1)} fusion(f32[2048,280]{1,0:T(8,128)} %get-tuple-element.124, f32[2048,280]{1,0:T(8,128)} %get-tuple-element.91, f32[2000]{0:T(1024)S(1)} %bitcast.58, bf16[512,280]{1,0:T(8,128)(2,1)S(1)} %get-tuple-element.109, bf16[512,280]{1,0:T(8,128)(2,1)S(1)} %get-tuple-element.110, f32[2000]{0:T(1024)S(1)} %bitcast.60, ...), kind=kLoop, calls=%fused_computation.44 | loop fusion | flops 7840000 | bytes 6770880 | tf_op jit(solution)/shard_map/convert_element_type | solution.py:450
  552.5 162.6 %all-reduce.7.cloned.1.call-done = (bf16[1120,840]{0,1:T(8,128)(2,1)}, bf16[280,1120]{1,0:T(8,128)(2,1)}, bf16[1120,1120]{1,0:T(8,128)(2,1)}, bf16[1120,1120]{1,0:T(8,128)(2,1)}) async-done(((bf16[1120,840]{0,1:T(8,128)(2,1)}, bf16[280,1120]{1,0:T(8,128)(2,1)}, bf16[1120,1120]{1,0:T(8,128)(2,1)}, bf16[1120,1120]{1,0:T(8,128)(2,1)}), (bf16[1120,840]{0,1:T(8,128)(2,1)}, bf16[280,1120]{1,0:T(8,128)(2,1)}, ...) | async-done | bytes 7526416 | tf_op jit(solution)/shard_map/psum | solution.py:431
  (314 shorter events, 212.3 us)
Async XLA Ops:
  7.2 231.7 %copy-start = (bf16[1120,1120]{1,0:T(8,128)(2,1)S(1)}, bf16[1120,1120]{1,0:T(8,128)(2,1)}, u32[]{:S(2)}) copy-start(bf16[1120,1120]{1,0:T(8,128)(2,1)} %param.27) | copy-start | bytes 7526404
  7.2 707.9 %all-reduce.7.cloned.1.call-start = ((), (), s32[]{:S(2)}) async-start(), calls=%async_computation | async-start | bytes 15482880 | tf_op jit(solution)/shard_map/psum | solution.py:431
  15.1 28.5 %collective-permute-start.1 = (bf16[2048,280]{0,1:T(8,128)(2,1)}, bf16[2048,280]{0,1:T(8,128)(2,1)}, u32[]{:S(2)}, u32[]{:S(2)}) collective-permute-start(bf16[2048,280]{0,1:T(8,128)(2,1)} %copy.87), channel_id=1, source_target_pairs={{0,2},{1,3},{2,0},{3,1},{4,6},{5,7},{6,4},{7,5},{8,10},{9,11},{10,... | collective-permute-start | bytes 3440648 | tf_op jit(solution)/shard_map/ppermute | solution.py:22
  18.1 33.3 %collective-permute-start = (bf16[2048,280]{0,1:T(8,128)(2,1)}, bf16[2048,280]{0,1:T(8,128)(2,1)}, u32[]{:S(2)}, u32[]{:S(2)}) collective-permute-start(bf16[2048,280]{0,1:T(8,128)(2,1)} %copy.87), channel_id=1, source_target_pairs={{0,1},{1,0},{2,3},{3,2},{4,5},{5,4},{6,7},{7,6},{8,9},{9,8},{10,11... | collective-permute-start | bytes 3440648 | tf_op jit(solution)/shard_map/ppermute | solution.py:22
  43.7 10.3 %collective-permute-start.2 = (bf16[2048,280]{0,1:T(8,128)(2,1)}, bf16[2048,280]{0,1:T(8,128)(2,1)}, u32[]{:S(2)}, u32[]{:S(2)}) collective-permute-start(bf16[2048,280]{0,1:T(8,128)(2,1)} %collective-permute-done.1), channel_id=1, source_target_pairs={{0,1},{1,0},{2,3},{3,2},{4,5},{5,4},{6,7},{7,6},{8,9},{9,8},{10,11... | collective-permute-start | bytes 3440648 | tf_op jit(solution)/shard_map/ppermute | solution.py:22
  43.8 3.7 collective-permute-start.4
  45.6 2.3 collective-permute-start.3
  47.5 1.2 collective-permute-start.5
  105.8 4.6 collective-permute-start.6
  125.3 28.4 %collective-permute-start.7 = (bf16[512,1120]{0,1:T(8,128)(2,1)}, bf16[512,1120]{0,1:T(8,128)(2,1)}, u32[]{:S(2)}, u32[]{:S(2)}) collective-permute-start(bf16[512,1120]{0,1:T(8,128)(2,1)} %copy.95), channel_id=1, source_target_pairs={{0,2},{1,3},{2,0},{3,1},{4,6},{5,7},{6,4},{7,5},{8,10},{9,11},{10,... | collective-permute-start | bytes 3440648 | tf_op jit(solution)/shard_map/ppermute | solution.py:22
  136.5 41.8 %collective-permute-start.14 = (bf16[2048,280]{0,1:T(8,128)(2,1)}, bf16[2048,280]{0,1:T(8,128)(2,1)}, u32[]{:S(2)}, u32[]{:S(2)}) collective-permute-start(bf16[2048,280]{0,1:T(8,128)(2,1)} %copy.113), channel_id=1, source_target_pairs={{0,2},{1,3},{2,0},{3,1},{4,6},{5,7},{6,4},{7,5},{8,10},{9,11},{10,... | collective-permute-start | bytes 3440648 | tf_op jit(solution)/shard_map/ppermute | solution.py:22
  164.1 38.0 %collective-permute-start.8 = (bf16[512,1120]{0,1:T(8,128)(2,1)}, bf16[512,1120]{0,1:T(8,128)(2,1)}, u32[]{:S(2)}, u32[]{:S(2)}) collective-permute-start(bf16[512,1120]{0,1:T(8,128)(2,1)} %copy.97), channel_id=1, source_target_pairs={{0,2},{1,3},{2,0},{3,1},{4,6},{5,7},{6,4},{7,5},{8,10},{9,11},{10,... | collective-permute-start | bytes 3440648 | tf_op jit(solution)/shard_map/ppermute | solution.py:22
  165.8 50.7 %collective-permute-start.13 = (bf16[2048,280]{0,1:T(8,128)(2,1)}, bf16[2048,280]{0,1:T(8,128)(2,1)}, u32[]{:S(2)}, u32[]{:S(2)}) collective-permute-start(bf16[2048,280]{0,1:T(8,128)(2,1)} %copy.113), channel_id=1, source_target_pairs={{0,1},{1,0},{2,3},{3,2},{4,5},{5,4},{6,7},{7,6},{8,9},{9,8},{10,11... | collective-permute-start | bytes 3440648 | tf_op jit(solution)/shard_map/ppermute | solution.py:22
  178.3 40.7 %collective-permute-start.15 = (bf16[2048,280]{0,1:T(8,128)(2,1)}, bf16[2048,280]{0,1:T(8,128)(2,1)}, u32[]{:S(2)}, u32[]{:S(2)}) collective-permute-start(bf16[2048,280]{0,1:T(8,128)(2,1)} %collective-permute-done.14), channel_id=1, source_target_pairs={{0,1},{1,0},{2,3},{3,2},{4,5},{5,4},{6,7},{7,6},{8,9},{9,8},{10,11... | collective-permute-start | bytes 3440648 | tf_op jit(solution)/shard_map/ppermute | solution.py:22
  178.3 55.5 %collective-permute-start.9 = (bf16[512,1120]{0,1:T(8,128)(2,1)}, bf16[512,1120]{0,1:T(8,128)(2,1)}, u32[]{:S(2)}, u32[]{:S(2)}) collective-permute-start(bf16[512,1120]{0,1:T(8,128)(2,1)} %copy.97), channel_id=1, source_target_pairs={{0,1},{1,0},{2,3},{3,2},{4,5},{5,4},{6,7},{7,6},{8,9},{9,8},{10,11... | collective-permute-start | bytes 3440648 | tf_op jit(solution)/shard_map/ppermute | solution.py:22
  202.1 34.1 %collective-permute-start.10 = (bf16[512,1120]{0,1:T(8,128)(2,1)}, bf16[512,1120]{0,1:T(8,128)(2,1)}, u32[]{:S(2)}, u32[]{:S(2)}) collective-permute-start(bf16[512,1120]{0,1:T(8,128)(2,1)} %collective-permute-done.8), channel_id=1, source_target_pairs={{0,1},{1,0},{2,3},{3,2},{4,5},{5,4},{6,7},{7,6},{8,9},{9,8},{10,11... | collective-permute-start | bytes 3440648 | tf_op jit(solution)/shard_map/ppermute | solution.py:22
  268.4 24.1 %collective-permute-start.16 = (bf16[1024,1120]{0,1:T(8,128)(2,1)}, bf16[1024,1120]{0,1:T(8,128)(2,1)}, u32[]{:S(2)}, u32[]{:S(2)}) collective-permute-start(bf16[1024,1120]{0,1:T(8,128)(2,1)} %convolution_convert_fusion.3), channel_id=1, source_target_pairs={{0,1},{1,0},{2,3},{3,2},{4,5},{5,4},{6,7},{7,6},{8,9},{9,8},{10,11... | collective-permute-start | bytes 6881288 | tf_op jit(solution)/shard_map/ppermute | solution.py:22
  284.7 34.8 %collective-permute-start.11 = (bf16[2048,560]{0,1:T(8,128)(2,1)}, bf16[2048,560]{0,1:T(8,128)(2,1)}, u32[]{:S(2)}, u32[]{:S(2)}) collective-permute-start(bf16[2048,560]{0,1:T(8,128)(2,1)} %copy.104), channel_id=1, source_target_pairs={{0,1},{1,0},{2,3},{3,2},{4,5},{5,4},{6,7},{7,6},{8,9},{9,8},{10,11... | collective-permute-start | bytes 6881288 | tf_op jit(solution)/shard_map/ppermute | solution.py:22
  305.0 27.5 %collective-permute-start.17 = (bf16[512,1120]{0,1:T(8,128)(2,1)}, bf16[512,1120]{0,1:T(8,128)(2,1)}, u32[]{:S(2)}, u32[]{:S(2)}) collective-permute-start(bf16[512,1120]{0,1:T(8,128)(2,1)} %copy.120), channel_id=1, source_target_pairs={{0,2},{1,3},{2,0},{3,1},{4,6},{5,7},{6,4},{7,5},{8,10},{9,11},{10,... | collective-permute-start | bytes 3440648 | tf_op jit(solution)/shard_map/ppermute | solution.py:22
  344.1 28.5 %collective-permute-start.18 = (bf16[512,1120]{0,1:T(8,128)(2,1)}, bf16[512,1120]{0,1:T(8,128)(2,1)}, u32[]{:S(2)}, u32[]{:S(2)}) collective-permute-start(bf16[512,1120]{0,1:T(8,128)(2,1)} %copy.122), channel_id=1, source_target_pairs={{0,2},{1,3},{2,0},{3,1},{4,6},{5,7},{6,4},{7,5},{8,10},{9,11},{10,... | collective-permute-start | bytes 3440648 | tf_op jit(solution)/shard_map/ppermute | solution.py:22
  362.1 33.2 %collective-permute-start.12 = (bf16[2048,280]{0,1:T(8,128)(2,1)}, bf16[2048,280]{0,1:T(8,128)(2,1)S(1)}, u32[]{:S(2)}, u32[]{:S(2)}) collective-permute-start(bf16[2048,280]{0,1:T(8,128)(2,1)} %copy.107), channel_id=1, source_target_pairs={{0,2},{1,3},{2,0},{3,1},{4,6},{5,7},{6,4},{7,5},{8,10},{9,11},{10,... | collective-permute-start | bytes 3440648 | tf_op jit(solution)/shard_map/ppermute | solution.py:22
  362.5 39.0 %collective-permute-start.19 = (bf16[512,1120]{0,1:T(8,128)(2,1)}, bf16[512,1120]{0,1:T(8,128)(2,1)}, u32[]{:S(2)}, u32[]{:S(2)}) collective-permute-start(bf16[512,1120]{0,1:T(8,128)(2,1)} %copy.122), channel_id=1, source_target_pairs={{0,1},{1,0},{2,3},{3,2},{4,5},{5,4},{6,7},{7,6},{8,9},{9,8},{10,11... | collective-permute-start | bytes 3440648 | tf_op jit(solution)/shard_map/ppermute | solution.py:22
  372.6 31.2 %collective-permute-start.20 = (bf16[512,1120]{0,1:T(8,128)(2,1)}, bf16[512,1120]{0,1:T(8,128)(2,1)}, u32[]{:S(2)}, u32[]{:S(2)}) collective-permute-start(bf16[512,1120]{0,1:T(8,128)(2,1)} %collective-permute-done.18), channel_id=1, source_target_pairs={{0,1},{1,0},{2,3},{3,2},{4,5},{5,4},{6,7},{7,6},{8,9},{9,8},{10,11... | collective-permute-start | bytes 3440648 | tf_op jit(solution)/shard_map/ppermute | solution.py:22
  460.0 15.7 %collective-permute-start.21 = (bf16[2048,560]{0,1:T(8,128)(2,1)}, bf16[2048,560]{0,1:T(8,128)(2,1)S(1)}, u32[]{:S(2)}, u32[]{:S(2)}) collective-permute-start(bf16[2048,560]{0,1:T(8,128)(2,1)} %convolution_convert_fusion.6), channel_id=1, source_target_pairs={{0,1},{1,0},{2,3},{3,2},{4,5},{5,4},{6,7},{7,6},{8,9},{9,8},{10,11... | collective-permute-start | bytes 6881288 | tf_op jit(solution)/shard_map/ppermute | solution.py:22
  468.8 25.0 %collective-permute-start.25 = (f32[2,1120]{1,0:T(2,128)S(1)}, f32[2,1120]{1,0:T(2,128)S(1)}, u32[]{:S(2)}, u32[]{:S(2)}) collective-permute-start(f32[2,1120]{1,0:T(2,128)S(1)} %pad_maximum_fusion.13), channel_id=1, source_target_pairs={{0,1},{1,0},{2,3},{3,2},{4,5},{5,4},{6,7},{7,6},{8,9},{9,8},{10,11... | collective-permute-start | bytes 26888 | tf_op jit(solution)/shard_map/ppermute | solution.py:22
  488.3 27.8 %collective-permute-start.22 = (bf16[2048,280]{0,1:T(8,128)(2,1)}, bf16[2048,280]{0,1:T(8,128)(2,1)}, u32[]{:S(2)}, u32[]{:S(2)}) collective-permute-start(bf16[2048,280]{0,1:T(8,128)(2,1)} %copy.130), channel_id=1, source_target_pairs={{0,2},{1,3},{2,0},{3,1},{4,6},{5,7},{6,4},{7,5},{8,10},{9,11},{10,... | collective-permute-start | bytes 3440648 | tf_op jit(solution)/shard_map/ppermute | solution.py:22
  493.8 22.2 %collective-permute-start.26 = (f32[2,1120]{1,0:T(2,128)S(1)}, f32[2,1120]{1,0:T(2,128)S(1)}, u32[]{:S(2)}, u32[]{:S(2)}) collective-permute-start(f32[2,1120]{1,0:T(2,128)S(1)} %fusion.84), channel_id=1, source_target_pairs={{0,2},{1,3},{2,0},{3,1},{4,6},{5,7},{6,4},{7,5},{8,10},{9,11},{10,... | collective-permute-start | bytes 26888 | tf_op jit(solution)/shard_map/ppermute | solution.py:22
  524.2 5.2 collective-permute-start.27
  529.4 4.3 collective-permute-start.28
  533.8 5.4 collective-permute-start.29
  533.8 5.4 collective-permute-start.23
  539.2 3.8 collective-permute-start.24
  (72 other events, 768.9 us)
Sparse Core Ops, SparseCore 0:
  462.8 252.3 all-reduce.6

commit v2 on v1

v2 whole, which is shorter than its diff:
```python
import functools

import jax
import jax.numpy as jnp
from jax import lax
from jax.experimental import pallas as pl
from jax.experimental.pallas import tpu as pltpu
from jax.sharding import PartitionSpec as P


D = 1120
HD = 56
EPS = 1e-05
BF = jnp.bfloat16
F32 = jnp.float32
QB = 256
SCALE = HD ** (-0.5)
MIB = 1 << 20


def swap(value, axis, mask):
    size = lax.axis_size(axis)
    return lax.ppermute(value, axis, [(i, i ^ mask) for i in range(size)])


def dot(left, right, dims=((1,), (0,))):
    return lax.dot_general(left, right, (dims, ((), ())), preferred_element_type=F32)


def gelu_tanh(values):
    return jax.nn.gelu(values, approximate=True)


def spot(rel):
    return (rel % 2) * 2 + rel // 2


def whole(shape):
    return pl.BlockSpec(shape, lambda i, *_: (0,) * len(shape), pipeline_mode=pl.Buffered(1))


def lanes(rows, width, where=None):
    return pl.BlockSpec((rows, width), (lambda i, s: (0, i)) if where is None else where)


def call(body, info, args, in_specs, outs, out_specs, steps, cost, scratch=(), vmem=40, alias=None):
    flops, moved = cost
    return pl.pallas_call(
        body,
        out_shape=outs,
        grid_spec=pltpu.PrefetchScalarGridSpec(
            num_scalar_prefetch=1,
            grid=(steps,),
            in_specs=in_specs,
            out_specs=out_specs,
            scratch_shapes=list(scratch),
        ),
        input_output_aliases=alias or {},
        compiler_params=pltpu.CompilerParams(
            dimension_semantics=("arbitrary",), vmem_limit_bytes=vmem * MIB
        ),
        cost_estimate=pl.CostEstimate(
            flops=int(flops), bytes_accessed=int(moved), transcendentals=0
        ),
    )(info, *args)


def array(*shape, dtype=BF):
    return jax.ShapeDtypeStruct(shape, dtype)


def place_features(info, parts, scratch, live=None):
    count = parts[0].shape[0]
    for rel in range(4):
        value = parts[rel][...].astype(F32)
        if live is not None:
            value = jnp.where(live, value, 0.0)
        start = pl.multiple_of((info[4] ^ rel) * count, 8)
        scratch[pl.ds(start, count), :] = value


def live_lanes(info, base, width):
    return base + lax.broadcasted_iota(jnp.int32, (1, width), 1) < info[3]


def first_of(rows, bounds):
    start = jnp.zeros_like(rows)
    for bound in bounds:
        start = jnp.where(rows >= bound, bound, start)
    return start


def window_blocks(bounds, step):
    return step - first_of(step * QB, bounds) // QB + 1


def allowed_keys(bounds, base, width):
    keys = base + QB - width + lax.broadcasted_iota(jnp.int32, (width, QB), 0)
    rows = base + lax.broadcasted_iota(jnp.int32, (1, QB), 1)
    return (keys >= first_of(rows, bounds)) & (keys <= rows)


def norm_rows(values):
    mean_row = jnp.sum(values, axis=0, keepdims=True) * (1.0 / D)
    centered = values - mean_row
    var_row = jnp.sum(centered * centered, axis=0, keepdims=True) * (1.0 / D)
    inv_row = lax.rsqrt(var_row + EPS)
    return (centered * inv_row, mean_row, inv_row)


def front_kernel(
    heads,
    info,
    own,
    near,
    far,
    cross,
    affine,
    wqkv,
    wout,
    normed,
    qkv,
    mixed,
    stats,
    keep,
    send,
    xmid,
    wide,
    kbuf,
    vtbuf,
    proj,
):
    step = pl.program_id(0)
    cols = heads * HD
    base = step * QB
    bounds = [info[k] for k in range(4)]
    count = window_blocks(bounds, step)
    here = pl.ds(pl.multiple_of(base, QB), QB)
    per = keep.shape[1] // 2 // QB
    rel = (step // per) ^ info[4]
    inner = step % per

    @pl.when(base >= bounds[3])
    def _():
        normed[...] = jnp.zeros_like(normed)
        qkv[...] = jnp.zeros_like(qkv)
        mixed[...] = jnp.zeros_like(mixed)
        stats[...] = jnp.zeros_like(stats)
        proj[...] = jnp.zeros_like(proj)
        wide[...] = jnp.zeros_like(wide)

    @pl.when(base < bounds[3])
    def _():
        place_features(info, (own, near, far, cross), wide, live_lanes(info, base, QB))
        hat, mean_row, inv_row = norm_rows(wide[...])
        stats[0:1, :] = mean_row
        stats[1:2, :] = inv_row
        normed[...] = (hat * affine[:, 0:1] + affine[:, 1:2]).astype(BF)
        joined = dot(wqkv[...], normed[...])
        qkv[...] = joined.astype(BF)
        for h in range(heads):
            keys = joined[cols + HD * h : cols + HD * (h + 1)]
            kbuf[h, here, :] = keys.T.astype(BF)
            vtbuf[h, :, here] = joined[2 * cols + HD * h : 2 * cols + HD * (h + 1)].astype(BF)
        for blocks in range(1, 4):

            @pl.when(count == blocks)
            def _(blocks=blocks):
                width = blocks * QB
                window = pl.ds(pl.multiple_of(base + QB - width, QB), width)
                allowed = allowed_keys(bounds, base, width)
                pieces = []
                for h in range(heads):
                    query = joined[HD * h : HD * (h + 1)].astype(BF)
                    scores = dot(kbuf[h, window, :], query) * SCALE
                    scores = jnp.where(allowed, scores, -1e30)
                    top = jnp.max(scores, axis=0, keepdims=True)
                    shifted = jnp.exp(scores - top)
                    total = jnp.sum(shifted, axis=0, keepdims=True)
                    weights = (shifted * (1.0 / total)).astype(BF)
                    pieces.append(dot(vtbuf[h, :, window], weights))
                    stats[2 + h : 3 + h, :] = top + jnp.log(total)
                mixed[...] = jnp.concatenate(pieces, axis=0).astype(BF)

        proj[...] = dot(wout[...], mixed[...]).astype(BF)

    target = pl.ds(pl.multiple_of((rel // 2) * (per * QB) + inner * QB, QB), QB)

    @pl.when(rel % 2 == 0)
    def _():
        keep[:, target] = proj[...]

    @pl.when(rel % 2 == 1)
    def _():
        send[:, target] = proj[...]

    @pl.when(rel == 0)
    def _():
        xmid[:, pl.ds(pl.multiple_of(inner * QB, QB), QB)] = wide[...].astype(BF)


def front(info, parts, affine, wqkv, wout, rows):
    joined, cols = wqkv.shape[0], wqkv.shape[0] // 3
    heads = cols // HD
    steps = rows // QB
    per = steps // 4

    def rel_lanes(i, s):
        return (0, spot((i // per) ^ s[4]) * per + i % per)

    return call(
        functools.partial(front_kernel, heads),
        info,
        (*parts, affine, wqkv, wout),
        [lanes(cols, QB)] * 4 + [whole((D, 4)), whole((joined, D)), whole((D, cols))],
        (
            array(D, rows),
            array(joined, rows),
            array(cols, rows),
            array(16, rows, dtype=F32),
            array(D, rows // 2),
            array(D, rows // 2),
            array(D, rows // 4),
        ),
        (
            lanes(D, QB),
            lanes(joined, QB),
            lanes(cols, QB, rel_lanes),
            lanes(16, QB),
            whole((D, rows // 2)),
            whole((D, rows // 2)),
            whole((D, rows // 4)),
        ),
        steps,
        (rows * D * 4 * cols * 4, rows * D * 20),
        [
            pltpu.VMEM((D, QB), F32),
            pltpu.VMEM((heads, rows, HD), BF),
            pltpu.VMEM((heads, HD, rows), BF),
            pltpu.VMEM((D, QB), BF),
        ],
    )


def add_kernel(info, left, right, out):
    out[...] = (left[...].astype(F32) + right[...].astype(F32)).astype(BF)


def fold_far(info, keep, got):
    rows = keep.shape[1] // 2
    step = 256
    shift = rows // step
    spec = lanes(D, step, lambda i, s: (0, i + shift))
    return call(
        add_kernel,
        info,
        (keep, got),
        [spec, spec],
        array(D, rows),
        lanes(D, step),
        rows // step,
        (rows * D, rows * D * 6),
    )


def middle_kernel(info, xmid, keep, got, last, affine, middle, normed, stats):
    values = xmid[...].astype(F32) + keep[...].astype(F32)
    values = values + got[...].astype(F32) + last[...].astype(F32)
    middle[...] = values
    hat, mean_row, inv_row = norm_rows(values)
    normed[...] = (hat * affine[:, 2:3] + affine[:, 3:4]).astype(BF)
    stats[...] = jnp.concatenate([mean_row, inv_row] * 4, axis=0)


def second_norm(info, xmid, keep, got, last, affine):
    rows = xmid.shape[1]
    step = 128
    return call(
        middle_kernel,
        info,
        (xmid, keep, got, last, affine),
        [lanes(D, step)] * 4 + [whole((D, 4))],
        (array(D, rows, dtype=F32), array(D, rows), array(8, rows, dtype=F32)),
        (lanes(D, step), lanes(D, step), lanes(8, step)),
        rows // step,
        (rows * D * 10, rows * D * 14),
    )


def cotangent_kernel(per, info, own, near, far, cross, out, wide):
    step = pl.program_id(0)
    place = step // per
    rel = (place % 2) * 2 + place // 2
    base = ((info[4] ^ rel) * per + step % per) * QB
    place_features(info, (own, near, far, cross), wide, live_lanes(info, base, QB))
    out[...] = wide[...].astype(BF)


def cotangent(info, parts, rows):
    steps = rows // QB
    per = steps // 4

    def natural(i, s):
        return (0, (s[4] ^ spot(i // per)) * per + i % per)

    return call(
        functools.partial(cotangent_kernel, per),
        info,
        parts,
        [lanes(parts[0].shape[0], QB, natural)] * 4,
        array(D, rows),
        lanes(D, QB),
        steps,
        (rows * D, rows * D * 6),
        [pltpu.VMEM((D, QB), F32)],
    )


def feed_kernel(
    first, per, info, n_one, n_two, g_rel, middle, wup_t, wup, wdown, wdown_t, *refs
):
    hidden, gpre, pn_one, pn_two, pd_keep, pd_send, now, act = refs[-8:]
    step = pl.program_id(0)
    rel = (0 if first else 2) + step // per
    base = ((info[4] ^ rel) * per + step % per) * QB
    cols = pd_keep.shape[0] // 2

    @pl.when(step < per)
    def _():
        now[...] = n_one[...]

    @pl.when(step >= per)
    def _():
        now[...] = n_two[...]

    @pl.when(base >= info[3])
    def _():
        for ref in (hidden, gpre, act, pd_keep, pd_send):
            ref[...] = jnp.zeros_like(ref)

    @pl.when(base < info[3])
    def _():
        pre = dot(wup_t[...], now[...])
        value, pull = jax.vjp(gelu_tanh, pre)
        hidden[...] = value.astype(BF)
        gpre[...] = pull(dot(wdown[...], g_rel[...]))[0].astype(BF)
        act[...] = dot(wup[...], gpre[...]).astype(BF)
        down = dot(wdown_t[...], hidden[...])
        if first:
            scale = jnp.where(step < per, 1.0, 0.0)
            for r, part in ((0, pd_keep), (2, pd_keep), (1, pd_send), (3, pd_send)):
                half = r // 2 * cols
                rows = pl.ds(pl.multiple_of((info[4] ^ r) * cols, 8), cols)
                start = half + (r % 2) * 2 * cols
                part[half : half + cols, :] = (
                    down[start : start + cols] + middle[rows, :] * scale
                ).astype(BF)
        else:
            pd_keep[...] = down[: 2 * cols].astype(BF)
            pd_send[...] = down[2 * cols :].astype(BF)

    @pl.when(step < per)
    def _():
        pn_one[...] = act[...]

    @pl.when(step >= per)
    def _():
        pn_two[...] = act[...]


def feed(info, first, n_one, n_two, g_rel, middle, weights, before=()):
    rows = g_rel.shape[1]
    steps = rows // QB // 2
    per = steps // 2
    cols = D // 4

    def place(i, s):
        return (0, ((i // per) * 2 + (0 if first else 1)) * per + i % per)

    low = lanes(D, QB, lambda i, s: (0, jnp.minimum(i, per - 1)))
    high = lanes(D, QB, lambda i, s: (0, jnp.maximum(i - per, 0)))
    spec = lanes(D, QB, place)
    half = lanes(2 * cols, QB, place)
    args = (n_one, n_two, g_rel, middle, *weights, *before)
    fixed = 4 + len(weights)
    return call(
        functools.partial(feed_kernel, first, per),
        info,
        args,
        [low, high, spec, low]
        + [whole((D, D))] * 4
        + [pl.BlockSpec(memory_space=pl.ANY)] * len(before),
        (
            array(D, rows),
            array(D, rows),
            array(D, rows // 4),
            array(D, rows // 4),
            array(2 * cols, rows),
            array(2 * cols, rows),
        ),
        (spec, spec, low, high, half, half),
        steps,
        (rows * D * D * 4, rows * D * 10 + D * D * 8),
        [pltpu.VMEM((D, QB), BF), pltpu.VMEM((D, QB), BF)],
        alias={fixed + 1 + k: out for k, out in enumerate((0, 1, 4, 5)[: len(before)])},
        vmem=48,
    )


def back_norm_kernel(info, keep, got, last, middle, stats, g_rel, affine, grad, sums):
    @pl.when(pl.program_id(0) == 0)
    def _():
        sums[...] = jnp.zeros_like(sums)

    total = keep[...].astype(F32) + got[...].astype(F32) + last[...].astype(F32)
    inv_row = stats[1:2, :]
    hat = (middle[...] - stats[0:1, :]) * inv_row
    scaled = total * affine[:, 2:3]
    product = scaled * hat
    mean_one = jnp.sum(scaled, axis=0, keepdims=True) * (1.0 / D)
    mean_two = jnp.sum(product, axis=0, keepdims=True) * (1.0 / D)
    grad[...] = (
        g_rel[...].astype(F32) + inv_row * (scaled - mean_one - hat * mean_two)
    ).astype(BF)
    sums[:, 0:1] += jnp.sum(total * hat, axis=1, keepdims=True)
    sums[:, 1:2] += jnp.sum(total, axis=1, keepdims=True)


def back_norm(info, keep, got, last, middle, stats, g_rel, affine):
    rows = middle.shape[1]
    step = 128
    return call(
        back_norm_kernel,
        info,
        (keep, got, last, middle, stats, g_rel, affine),
        [lanes(D, step)] * 4 + [lanes(8, step), lanes(D, step), whole((D, 4))],
        (array(D, rows), array(D, 2, dtype=F32)),
        (lanes(D, step), whole((D, 2))),
        rows // step,
        (rows * D * 20, rows * D * 14),
    )


def back_kernel(
    heads,
    info,
    own,
    near,
    far,
    cross,
    qkv,
    qkv_now,
    stats,
    wout,
    wqkv,
    joined,
    keep,
    send,
    gown,
    now,
    wide,
    kbuf,
    vbuf,
    ktbuf,
    dkbuf,
    dvbuf,
):
    steps = pl.num_programs(0)
    step = steps - 1 - pl.program_id(0)
    cols = heads * HD
    base = step * QB
    bounds = [info[k] for k in range(4)]
    count = window_blocks(bounds, step)
    here = pl.ds(pl.multiple_of(base, QB), QB)
    rel = (step // (steps // 4)) ^ info[4]

    @pl.when(pl.program_id(0) == 0)
    def _():
        dkbuf[...] = jnp.zeros_like(dkbuf)
        dvbuf[...] = jnp.zeros_like(dvbuf)
        for h in range(heads):
            keys = qkv[cols + HD * h : cols + HD * (h + 1), :]
            ktbuf[h] = keys
            kbuf[h] = keys.T
            vbuf[h] = qkv[2 * cols + HD * h : 2 * cols + HD * (h + 1), :].T

    for r, part in enumerate((own, near, far, cross)):

        @pl.when(rel == r)
        def _(part=part):
            now[...] = part[...]

    wide[...] = now[...].astype(F32)
    gown[...] = wide[pl.ds(pl.multiple_of(info[4] * cols, 8), cols), :].astype(BF)

    @pl.when(base >= bounds[3])
    def _():
        for ref in (joined, keep, send):
            ref[...] = jnp.zeros_like(ref)

    @pl.when(base < bounds[3])
    def _():
        gmix = dot(wout[...], now[...])
        for blocks in range(1, 4):

            @pl.when(count == blocks)
            def _(blocks=blocks):
                width = blocks * QB
                window = pl.ds(pl.multiple_of(base + QB - width, QB), width)
                allowed = allowed_keys(bounds, base, width)
                for h in range(heads):
                    query = qkv_now[HD * h : HD * (h + 1), :]
                    grads = gmix[HD * h : HD * (h + 1)].astype(BF)
                    scores = dot(kbuf[h, window, :], query) * SCALE
                    probs = jnp.exp(
                        jnp.where(allowed, scores, -1e30) - stats[2 + h : 3 + h, :]
                    )
                    grad_probs = dot(vbuf[h, window, :], grads)
                    dvbuf[h, :, window] += dot(grads, probs.astype(BF), ((1,), (1,)))
                    delta = jnp.sum(probs * grad_probs, axis=0, keepdims=True)
                    grad_scores = (probs * (grad_probs - delta) * SCALE).astype(BF)
                    dkbuf[h, :, window] += dot(query, grad_scores, ((1,), (1,)))
                    wide[HD * h : HD * (h + 1), :] = dot(ktbuf[h, :, window], grad_scores)

        for h in range(heads):
            wide[cols + HD * h : cols + HD * (h + 1), :] = dkbuf[h, :, here]
            wide[2 * cols + HD * h : 2 * cols + HD * (h + 1), :] = dvbuf[h, :, here]
        joined[...] = wide[: 3 * cols, :].astype(BF)
        partial = dot(wqkv[...], joined[...])
        keep[...] = partial[: 2 * cols].astype(BF)
        send[...] = partial[2 * cols :].astype(BF)


def back(info, parts, qkv, stats, wout, wqkv):
    rows = qkv.shape[1]
    joined, cols = qkv.shape[0], qkv.shape[0] // 3
    heads = cols // HD
    steps = rows // QB
    per = steps // 4

    def turn(i, s):
        return (0, steps - 1 - i)

    def part_spec(r):
        def where(i, s):
            step = steps - 1 - i
            return (0, jnp.where((step // per) ^ s[4] == r, step % per, 0))

        return lanes(D, QB, where)

    return call(
        functools.partial(back_kernel, heads),
        info,
        (*parts, qkv, qkv, stats, wout, wqkv),
        [part_spec(r) for r in range(4)]
        + [whole((joined, rows)), lanes(joined, QB, turn), lanes(16, QB, turn)]
        + [whole((cols, D)), whole((D, joined))],
        (array(joined, rows), array(2 * cols, rows), array(2 * cols, rows), array(cols, rows)),
        (
            lanes(joined, QB, turn),
            lanes(2 * cols, QB, turn),
            lanes(2 * cols, QB, turn),
            lanes(cols, QB, turn),
        ),
        steps,
        (rows * D * 4 * cols * 6, rows * D * 20),
        [
            pltpu.VMEM((D, QB), BF),
            pltpu.VMEM((D, QB), F32),
            pltpu.VMEM((heads, rows, HD), BF),
            pltpu.VMEM((heads, rows, HD), BF),
            pltpu.VMEM((heads, HD, rows), BF),
            pltpu.VMEM((heads, HD, rows), F32),
            pltpu.VMEM((heads, HD, rows), F32),
        ],
        vmem=48,
    )


def column_maps(per, relative, row):
    def mine(i, s):
        return (row, spot((i // per) ^ s[4]) * per + i % per if relative else i)

    def near(i, s):
        return (row, spot((i // per) ^ s[4] ^ 1) * per + i % per if relative else i)

    return (mine, near)


def fold_columns_far(info, keep, got, relative):
    cols, rows = keep.shape[0] // 2, keep.shape[1]
    steps = rows // QB
    mine, near = column_maps(steps // 4, relative, 1)
    return call(
        add_kernel,
        info,
        (keep, got),
        [lanes(cols, QB, mine), lanes(cols, QB, near)],
        array(cols, rows),
        lanes(cols, QB),
        steps,
        (rows * cols, rows * cols * 6),
    )


def out_kernel(info, keep, got, last, out):
    total = keep[...].astype(F32) + got[...].astype(F32) + last[...].astype(F32)
    live = live_lanes(info, pl.program_id(0) * QB, QB)
    out[...] = jnp.where(live, total, 0.0).astype(BF)


def out_rows(info, keep, got, last, home_rows):
    cols, rows = last.shape
    steps = rows // QB
    mine, near = column_maps(steps // 4, True, 0)
    return call(
        out_kernel,
        info,
        (keep, got, last),
        [lanes(cols, QB, mine), lanes(cols, QB, near), lanes(cols, QB)],
        array(cols, home_rows),
        lanes(cols, QB),
        steps,
        (rows * cols * 4, rows * cols * 8),
    )


def first_sums_kernel(info, keep, got, last, x, stats, gain, total, rowsums, sums):
    @pl.when(pl.program_id(0) == 0)
    def _():
        sums[...] = jnp.zeros_like(sums)

    live = live_lanes(info, pl.program_id(0) * QB, QB)
    grad = keep[...].astype(F32) + got[...].astype(F32) + last[...].astype(F32)
    grad = jnp.where(live, grad, 0.0)
    hat = (jnp.where(live, x[...].astype(F32), 0.0) - stats[0:1, :]) * stats[1:2, :]
    scaled = grad * gain[:, 0:1]
    total[...] = grad
    one = jnp.sum(scaled, axis=0, keepdims=True)
    two = jnp.sum(scaled * hat, axis=0, keepdims=True)
    rowsums[...] = jnp.concatenate([one, two] * 4, axis=0)
    sums[:, 0:1] += jnp.sum(grad * hat, axis=1, keepdims=True)
    sums[:, 1:2] += jnp.sum(grad, axis=1, keepdims=True)


def first_sums(info, keep, got, last, x, stats, gain):
    cols, rows = last.shape
    top = lanes(cols, QB)
    return call(
        first_sums_kernel,
        info,
        (keep, got, last, x, stats, gain),
        [top, top, top, top, lanes(16, QB), whole((cols, 2))],
        (array(cols, rows, dtype=F32), array(8, rows, dtype=F32), array(cols, 2, dtype=F32)),
        (top, lanes(8, QB), whole((cols, 2))),
        rows // QB,
        (rows * cols * 10, rows * cols * 14),
    )


def x_grad_kernel(info, total, rowsums, x, stats, gain, gown, out):
    live = live_lanes(info, pl.program_id(0) * QB, QB)
    inv_row = stats[1:2, :]
    hat = (jnp.where(live, x[...].astype(F32), 0.0) - stats[0:1, :]) * inv_row
    inner = total[...] * gain[:, 0:1] - rowsums[0:1, :] * (1.0 / D)
    inner = inner - hat * (rowsums[1:2, :] * (1.0 / D))
    grad = gown[...].astype(F32) + inv_row * inner
    out[...] = jnp.where(live, grad, 0.0).astype(BF)


def x_gradient(info, total, rowsums, x, stats, gain, gown, home_rows):
    cols, rows = total.shape
    top = lanes(cols, QB)
    return call(
        x_grad_kernel,
        info,
        (total, rowsums, x, stats, gain, gown),
        [top, lanes(8, QB), top, lanes(16, QB), whole((cols, 2)), top],
        array(cols, home_rows),
        top,
        rows // QB,
        (rows * cols * 10, rows * cols * 14),
    )


def gather_parts(value):
    near = swap(value, "tensor", 1)
    far = swap(value, "tensor", 2)
    return (value, near, far, swap(far, "tensor", 1))


def total_over(value, axis):
    mask = 1
    while mask < lax.axis_size(axis):
        value = value + swap(value, axis, mask)
        mask *= 2
    return value


def sum_groups(value, group):
    halved = []
    mask = 1
    while mask < lax.axis_size("dp"):
        if len(halved) < 2:
            half = value.shape[0] // 2
            bit = (group // mask) % 2
            got = swap(lax.dynamic_slice_in_dim(value, (1 - bit) * half, half), "dp", mask)
            mine = lax.dynamic_slice_in_dim(value, bit * half, half)
            halved.append((mask, bit))
        else:
            got, mine = swap(value, "dp", mask), value
        value = (mine.astype(F32) + got.astype(F32)).astype(BF)
        mask *= 2
    for mask, bit in reversed(halved):
        other = swap(value, "dp", mask)
        low = bit == 0
        value = jnp.concatenate([jnp.where(low, value, other), jnp.where(low, other, value)])
    return value


def shards(
    x_home,
    cot_home,
    cell_len,
    norm1_gain,
    norm1_bias,
    qkv_weight,
    out_weight,
    norm2_gain,
    norm2_bias,
    up_weight,
    down_weight,
):
    groups = cell_len.shape[0]
    home_rows, cols = x_home.shape
    rows = -(-home_rows // 1024) * 1024
    me = lax.axis_index("tensor").astype(jnp.int32)
    group = lax.axis_index("dp")
    weight = groups / jnp.sum(cell_len).astype(F32)
    my_len = lax.dynamic_index_in_dim(cell_len, group, 0, keepdims=False)
    bounds = jnp.cumsum(my_len).astype(jnp.int32)
    info = jnp.concatenate([bounds, jnp.broadcast_to(me, (4,))])
    order = (me, me ^ 2, me ^ 1, me ^ 3)

    x = x_home.T
    x_parts = gather_parts(x)
    cot_parts = gather_parts(cot_home.T)
    own_affine = jnp.stack([norm1_gain, norm1_bias, norm2_gain, norm2_bias], axis=1)
    stacked = jnp.stack(gather_parts(own_affine))
    affine = jnp.concatenate(
        [lax.dynamic_index_in_dim(stacked, me ^ j, 0, keepdims=False) for j in range(4)]
    )

    def rel_rows(value):
        return jnp.concatenate([lax.dynamic_slice_in_dim(value, j * cols, cols) for j in order])

    wqkv_t = qkv_weight.transpose(1, 2, 0).reshape(3 * cols, D)
    wqkv = rel_rows(qkv_weight.reshape(D, 3 * cols))
    wout_t = out_weight.T
    wup_t = up_weight.T
    wdown_t = rel_rows(down_weight.T)

    normed, qkv, mixed, stats, keep, send, xmid = front(info, x_parts, affine, wqkv_t, wout_t, rows)
    got = swap(send, "tensor", 1)
    last = swap(fold_far(info, keep, got), "tensor", 2)
    middle, n_own, stats_two = second_norm(info, xmid, keep, got, last, affine)
    n_own, n_near, n_far, n_cross = gather_parts(n_own)

    g_rel = cotangent(info, cot_parts, rows)
    weights = (wup_t, up_weight, down_weight, wdown_t)
    hidden, gpre, pn_own, pn_near, pd_keep, pd_send = feed(
        info, True, n_own, n_near, g_rel, middle, weights
    )
    hidden, gpre, pn_far, pn_cross, pd_keep, pd_send = feed(
        info, False, n_far, n_cross, g_rel, middle, weights, (hidden, gpre, pd_keep, pd_send)
    )
    got_own = swap(pn_near, "tensor", 1)
    got_far = swap(pn_cross, "tensor", 1)
    far_sum = call(
        add_kernel,
        info,
        (pn_far, got_far),
        [lanes(D, QB)] * 2,
        array(D, rows // 4),
        lanes(D, QB),
        rows // 4 // QB,
        (rows * D // 4, rows * D * 3 // 2),
    )
    last = swap(far_sum, "tensor", 2)
    grad_mid, sums_two = back_norm(
        info, pn_own, got_own, last, middle, stats_two, g_rel, affine
    )
    g_parts = gather_parts(grad_mid)

    rows_dims = ((1,), (1,))
    n_rel = jnp.concatenate([n_own, n_far, n_near, n_cross], axis=1)
    grad_down = sum_groups(dot(hidden, g_rel, rows_dims).astype(BF), group)
    grad_up = sum_groups(dot(n_rel, gpre, rows_dims).astype(BF), group)

    joined, keep, send, gown = back(info, g_parts, qkv, stats, out_weight, wqkv)
    gm_rel = jnp.concatenate([g_parts[0], g_parts[2], g_parts[1], g_parts[3]], axis=1)
    grad_rest = jnp.concatenate([dot(joined, normed, rows_dims), dot(mixed, gm_rel, rows_dims)])
    grad_rest = sum_groups(grad_rest.astype(BF), group)

    got = swap(send, "tensor", 1)
    last = swap(fold_columns_far(info, keep, got, False), "tensor", 2)
    total, rowsums, sums_one = first_sums(info, keep, got, last, x, stats, own_affine[:, :2])
    rowsums = total_over(rowsums, "tensor")
    x_grad = x_gradient(info, total, rowsums, x, stats, own_affine[:, :2], gown, home_rows)

    got = swap(pd_send, "tensor", 1)
    last = swap(fold_columns_far(info, pd_keep, got, True), "tensor", 2)
    out = out_rows(info, pd_keep, got, last, home_rows)

    sums_two = lax.dynamic_slice_in_dim(total_over(sums_two, "tensor"), me * cols, cols)
    small = total_over(jnp.concatenate([sums_one, sums_two], axis=1), "dp") * weight

    def scaled(item):
        return item.astype(F32) * weight

    grad_qkv = scaled(grad_rest[: 3 * cols]).reshape(3, cols, D).transpose(2, 0, 1)
    return (
        out.T,
        x_grad.T,
        small[:, 0],
        small[:, 1],
        grad_qkv,
        scaled(grad_rest[3 * cols :]),
        small[:, 2],
        small[:, 3],
        scaled(grad_up),
        scaled(grad_down),
    )


def solution(mesh):
    rows, vector = P("dp", "tensor"), P("tensor")
    qkv, wide, tall = P(None, None, "tensor"), P(None, "tensor"), P("tensor", None)
    return jax.shard_map(
        shards,
        mesh=mesh,
        in_specs=(rows, rows, P(), vector, vector, qkv, tall, vector, vector, wide, tall),
        out_specs=(rows, rows, vector, vector, qkv, tall, vector, vector, wide, tall),
        check_vma=False,
    )
```

time: 736 us -> 536 us (0.73)
  waiting for transfers between devices: 300 us -> 212 us
  local copies, waits for them, and re-layouts: 141 us -> 54.3 us
  matrix products: 114 us -> 28.5 us
  Pallas kernels: 70.4 us -> 151 us
  other arithmetic: 70.9 us -> 41.8 us
  starting transfers between devices: 18.8 us -> 36.1 us
  between operations: 18.7 us -> 2.4 us
    psum x1 -> x0, waiting for transfers between devices: 163 us -> none  [shards(): grad_qkv, grad_out_w = lax.psum((grad_qkv, grad_out_w), 'dp')]
    dot_general x16 -> x4, matrix products: 114 us -> 28.5 us  [dot(): lax.dot_general(left, right, (dims, ((), ())), preferred_element_type=F32)]
    pallas_call x4 -> x14, Pallas kernels: 70.4 us -> 151 us  [call(): pl.pallas_call(body, out_shape=outs, grid_spec=pltpu.PrefetchScalarGridSp...]
    ppermute x30 -> x46, waiting for transfers between devices: 137 us -> 212 us  [swap(): return lax.ppermute(value, axis, [(i, i ^ mask) for i in range(size)])]
    ppermute x15 -> x1, local copies, waits for them, and re-layouts: 36.3 us -> 0.24 us  [swap(): return lax.ppermute(value, axis, [(i, i ^ mask) for i in range(size)])]
    convert_element_type x6 -> x0, local copies, waits for them, and re-layouts: 22 us -> none  [the longest x2 9.48 us: fold_rows(): both = keep + got.astype(F32)]
    reduce_sum x6 -> x0, other arithmetic: 19.8 us -> none  [the longest x1 5.44 us: shards(): jnp.sum(a_one, axis=1)]
    ppermute x30 -> x46, starting transfers between devices: 18.7 us -> 36.1 us  [swap(): return lax.ppermute(value, axis, [(i, i ^ mask) for i in range(size)])]
  transfers between devices with their start and end apart: 31 -> 46, of which waited for: 15 -> 21; matrix products, arithmetic and copies ran while one was open for 26% -> 18% of each run, Pallas kernels for 0% -> 18%
where the time goes in v2:
time: 536 us; the launch traced here: 526 us
  waiting for transfers between devices  212 us (40%)
  Pallas kernels  151 us (28%)
  local copies, waits for them, and re-layouts  54.3 us (10%)
  other arithmetic  41.8 us (8%)
  starting transfers between devices  36.1 us (7%)
  matrix products  28.5 us (5%)
    ppermute x46, waiting for transfers between devices, swap(): return lax.ppermute(value, axis, [(i, i ^ mask) for i in range(size)])  212 us
    pallas_call x14, Pallas kernels, call(): pl.pallas_call(body, out_shape=outs, grid_spec=pltpu.PrefetchScalarGridSp...  151 us
    ppermute x46, starting transfers between devices, swap(): return lax.ppermute(value, axis, [(i, i ^ mask) for i in range(size)])  36.1 us
    unnamed x113, local copies, waits for them, and re-layouts  33.8 us
    dot_general x4, matrix products, dot(): lax.dot_general(left, right, (dims, ((), ())), preferred_element_type=F32)  28.5 us
    convert_element_type x9, other arithmetic, sum_groups(): value = (mine.astype(F32) + got.astype(F32)).astype(BF)  13.5 us
  transfers between devices with their start and end apart: 46, of which 21 were waited for; matrix products, arithmetic and copies ran while one was open for 18% of the time, Pallas kernels for 18%

profile of v2, /device:TPU:0, one launch (start us, length us, event | category | flops | bytes accessed | tf_op | source)
XLA Modules:
  0.0 526.4 jit_solution(18235196062179578836)
XLA Ops:
  3.7 25.6 %collective-permute-done.1.far = bf16[280,2000]{1,0:T(8,128)(2,1)} collective-permute-done((bf16[280,2000]{1,0:T(8,128)(2,1)}, bf16[280,2000]{1,0:T(8,128)(2,1)}, u32[]{:S(2)}, u32[]{:S(2)}) %collective-permute-start.1) | collective-permute-done | bytes 1120032 | tf_op jit(solution)/shard_map/ppermute | solution.py:23
  40.3 32.4 %shard_map.186 = (bf16[1120,2048]{1,0:T(8,128)(2,1)}, bf16[840,2048]{1,0:T(8,128)(2,1)}, bf16[280,2048]{1,0:T(8,128)(2,1)S(1)}, f32[16,2048]{1,0:T(8,128)S(1)}, ...) custom-call(s32[8]{0:T(128)S(1)} %concatenate.44.info, ...), custom_call_target="tpu_custom_call" | custom-call | flops 10276044800 | bytes 45875200 | tf_op jit(solution)/shard_map/pallas_call | solution.py:48
  73.2 4.3 collective-permute-done.6.right.got
  80.9 26.1 %collective-permute-done.7.last = bf16[1120,512]{1,0:T(8,128)(2,1)S(1)} collective-permute-done((bf16[1120,512]{1,0:T(8,128)(2,1)S(1)}, bf16[1120,512]{1,0:T(8,128)(2,1)S(1)}, u32[]{:S(2)}, u32[]{:S(2)}) %collective-permute-start.7) | collective-permute-done | bytes 1146912 | tf_op jit(solution)/shard_map/ppermute | solution.py:23
  106.9 5.9 %shard_map.188 = (f32[1120,512]{1,0:T(8,128)S(1)}, bf16[1120,512]{1,0:T(8,128)(2,1)}, f32[8,512]{1,0:T(8,128)S(1)}) custom-call(s32[8]{0:T(128)S(1)} %concatenate.44.info, bf16[1120,512]{1,0:T(8,128)(2,1)S(1)} %get-tuple-element.41.xmid, bf16[1120,1024]{1,0:T(8,128)(2,1)S(1)} %get-tuple-element.42.left.keep, ...), custom_call_target="tpu_custom_call" | custom-call | flops 5734400 | bytes 8028160 | tf_op jit(solution)/shard_map/pallas_call | solution.py:48
  116.5 15.0 %collective-permute-done.11.far = bf16[280,2000]{1,0:T(8,128)(2,1)S(1)} collective-permute-done((bf16[280,2000]{1,0:T(8,128)(2,1)S(1)}, bf16[280,2000]{1,0:T(8,128)(2,1)S(1)}, u32[]{:S(2)}, u32[]{:S(2)}) %collective-permute-start.11) | collective-permute-done | bytes 1120032 | tf_op jit(solution)/shard_map/ppermute | solution.py:23
  131.5 6.1 %constant_dynamic-slice_fusion.13 = (bf16[1120,280]{1,0:T(8,128)(2,1)}, bf16[1120,280]{1,0:T(8,128)(2,1)}, bf16[1120,280]{1,0:T(8,128)(2,1)}, bf16[1120,280]{1,0:T(8,128)(2,1)}) fusion(bf16[1120,1120]{1,0:T(8,128)(2,1)} %wdown.3, s32[]{:T(128)S(6)} %select_n.143, s32[]{:T(128)S(6)} %select_n.145, s32[]{:T(128)S(6)} %select_n.144, s32[]{:T(128)S(6)} %select_n.146), kind=kLoop, calls=%fused_computation.71 | loop fusion | bytes 5017616 | tf_op jit(solution)/shard_map/dynamic-slice
  145.9 9.8 %collective-permute-done.8.n_one = bf16[1120,512]{1,0:T(8,128)(2,1)} collective-permute-done((bf16[1120,512]{1,0:T(8,128)(2,1)}, bf16[1120,512]{1,0:T(8,128)(2,1)}, u32[]{:S(2)}, u32[]{:S(2)}) %collective-permute-start.8) | collective-permute-done | bytes 1146912 | tf_op jit(solution)/shard_map/ppermute | solution.py:23
  158.9 5.2 copy.51
  164.1 6.1 %shard_map.189.g_rel = bf16[1120,2048]{1,0:T(8,128)(2,1)S(1)} custom-call(s32[8]{0:T(128)S(1)} %concatenate.44.info, bf16[280,2000]{1,0:T(8,128)(2,1)S(1)} %bitcast.49, bf16[280,2000]{1,0:T(8,128)(2,1)} %collective-permute-done.10.near, bf16[280,2000]{1,0:T(8,128)(2,1)S(1)} %collective-permute-done.11.far, bf16[280,2000]{1,0:T(8,128)(2,1)} %collective-permute-done.12.cross), custom_call_target="tpu_custom_call" | custom-call | flops 2293760 | bytes 13762560 | tf_op jit(solution)/shard_map/pallas_call | solution.py:48
  172.4 22.6 %shard_map.190 = (bf16[1120,2048]{1,0:T(8,128)(2,1)}, bf16[1120,2048]{1,0:T(8,128)(2,1)}, bf16[1120,512]{1,0:T(8,128)(2,1)S(1)}, bf16[1120,512]{1,0:T(8,128)(2,1...) custom-call(s32[8]{0:T(128)S(1)} %concatenate.44.info, bf16[1120,512]{1,0:T(8,128)(2,1)} %get-tuple-element.44.n_one, ...), custom_call_target="tpu_custom_call" | custom-call | flops 10276044800 | bytes 32972800 | tf_op jit(solution)/shard_map/pallas_call | solution.py:48
  195.0 16.9 %shard_map.191 = (bf16[1120,2048]{1,0:T(8,128)(2,1)}, bf16[1120,2048]{1,0:T(8,128)(2,1)}, bf16[1120,512]{1,0:T(8,128)(2,1)S(1)}, bf16[1120,512]{1,0:T(8,128)(2,1...) custom-call(s32[8]{0:T(128)S(1)} %concatenate.44.info, ...), custom_call_target="tpu_custom_call", output_to_operand_aliasing={{0}: (9, {}), {1}: (10, {}), {4}: (11, {}), {5}: (12, {})} | custom-call | flops 10276044800 | bytes 32972800 | tf_op jit(solution)/shard_map/pallas_call | solution.py:48
  212.0 9.7 %convolution_convert_fusion.1 = bf16[1120,1120]{1,0:T(8,128)(2,1)S(1)} fusion(bf16[1120,2048]{1,0:T(8,128)(2,1)} %get-tuple-element.70, bf16[1120,512]{1,0:T(8,128)(2,1)} %collective-permute-done.9.n_two, bf16[1120,512]{1,0:T(8,128)(2,1)} %collective-permute-done.13.n_two, bf16[1120,512]{1,0:T(8,128)(2,1)} %collective-permute-done.8.n_one, ...), kind=kOutput, calls=%fused_computation.1 | convolution fusion | flops 5157626880 | bytes 11683840 | tf_op jit(solution)/shard_map/dot_general | solution.py:27
  223.5 6.4 %convolution_convert_fusion = bf16[1120,1120]{1,0:T(8,128)(2,1)S(1)} fusion(bf16[1120,2048]{1,0:T(8,128)(2,1)S(1)} %copy-done.48, bf16[1120,2048]{1,0:T(8,128)(2,1)S(1)} %bitcast.39), kind=kOutput, calls=%fused_computation | convolution fusion | flops 5139276800 | bytes 11683840 | tf_op jit(solution)/shard_map/dot_general | solution.py:27
  245.5 8.9 %collective-permute-done.36 = bf16[560,1120]{1,0:T(8,128)(2,1)} collective-permute-done((bf16[560,1120]{1,0:T(8,128)(2,1)}, bf16[560,1120]{1,0:T(8,128)(2,1)}, u32[]{:S(2)}, u32[]{:S(2)}) %collective-permute-start.36) | collective-permute-done | bytes 1254432 | tf_op jit(solution)/shard_map/ppermute | solution.py:23
  264.8 6.1 %shard_map.195 = (bf16[1120,512]{1,0:T(8,128)(2,1)}, f32[1120,2]{1,0:T(8,128)S(1)}) custom-call(s32[8]{0:T(128)S(1)} %concatenate.44.info, bf16[1120,512]{1,0:T(8,128)(2,1)S(1)} %copy-done.17, bf16[1120,512]{1,0:T(8,128)(2,1)} %collective-permute-done.16.got, bf16[1120,512]{1,0:T(8,128)(2,1)} %collective-permute-done.18.last, f32[1120,512]{1,0:T(8,128)S(1)} %copy-done.10, ...), custom_call_target="tpu_custom_call" | custom-call | flops 11468800 | bytes 8028160 | tf_op jit(solution)/shard_map/pallas_call | solution.py:48
  272.6 8.6 %collective-permute-done.41 = bf16[560,1120]{1,0:T(8,128)(2,1)} collective-permute-done((bf16[560,1120]{1,0:T(8,128)(2,1)}, bf16[560,1120]{1,0:T(8,128)(2,1)}, u32[]{:S(2)}, u32[]{:S(2)}) %collective-permute-start.41) | collective-permute-done | bytes 1254432 | tf_op jit(solution)/shard_map/ppermute | solution.py:23
  286.5 11.3 %collective-permute-done.20.far = bf16[1120,512]{1,0:T(8,128)(2,1)} collective-permute-done((bf16[1120,512]{1,0:T(8,128)(2,1)}, bf16[1120,512]{1,0:T(8,128)(2,1)}, u32[]{:S(2)}, u32[]{:S(2)}) %collective-permute-start.20) | collective-permute-done | bytes 1146912 | tf_op jit(solution)/shard_map/ppermute | solution.py:23
  299.6 5.3 %collective-permute-done.42 = bf16[280,1120]{1,0:T(8,128)(2,1)} collective-permute-done((bf16[280,1120]{1,0:T(8,128)(2,1)}, bf16[280,1120]{1,0:T(8,128)(2,1)}, u32[]{:S(2)}, u32[]{:S(2)}) %collective-permute-start.42) | collective-permute-done | bytes 627232 | tf_op jit(solution)/shard_map/ppermute | solution.py:23
  319.1 13.7 %collective-permute-done.38 = bf16[280,1120]{1,0:T(8,128)(2,1)} collective-permute-done((bf16[280,1120]{1,0:T(8,128)(2,1)}, bf16[280,1120]{1,0:T(8,128)(2,1)}, u32[]{:S(2)}, u32[]{:S(2)}) %collective-permute-start.38) | collective-permute-done | bytes 627232 | tf_op jit(solution)/shard_map/ppermute | solution.py:23
  335.8 33.4 %shard_map.196 = (bf16[840,2048]{1,0:T(8,128)(2,1)}, bf16[560,2048]{1,0:T(8,128)(2,1)}, bf16[560,2048]{1,0:T(8,128)(2,1)}, bf16[280,2048]{1,0:T(8,128)(2,1)S(1)}) custom-call(s32[8]{0:T(128)S(1)} %concatenate.44.info, bf16[1120,512]{1,0:T(8,128)(2,1)} %get-tuple-element.57.own, bf16[1120,512]{1,0:T(8,128)(2,1)} %collective-permute-done.19.near, ...), custom_call_target="tpu_custom_call" | custom-call | flops 15414067200 | bytes 45875200 | tf_op jit(solution)/shard_map/pallas_call | solution.py:48
  369.2 8.4 %convolution_convert_fusion.2 = bf16[840,1120]{1,0:T(8,128)(2,1)S(1)} fusion(bf16[840,2048]{1,0:T(8,128)(2,1)} %get-tuple-element.67, bf16[1120,2048]{1,0:T(8,128)(2,1)} %get-tuple-element.68), kind=kOutput, calls=%fused_computation.20 | convolution fusion | flops 3854457600 | bytes 9909760 | tf_op jit(solution)/shard_map/dot_general | solution.py:27
  389.9 24.4 %collective-permute-done.31 = bf16[560,1120]{1,0:T(8,128)(2,1)S(1)} collective-permute-done((bf16[560,1120]{1,0:T(8,128)(2,1)S(1)}, bf16[560,1120]{1,0:T(8,128)(2,1)S(1)}, u32[]{:S(2)}, u32[]{:S(2)}) %collective-permute-start.31) | collective-permute-done | bytes 1254432 | tf_op jit(solution)/shard_map/ppermute | solution.py:23
  419.1 13.8 %collective-permute-done.32 = bf16[280,1120]{1,0:T(8,128)(2,1)S(1)} collective-permute-done((bf16[280,1120]{1,0:T(8,128)(2,1)S(1)}, bf16[280,1120]{1,0:T(8,128)(2,1)S(1)}, u32[]{:S(2)}, u32[]{:S(2)}) %collective-permute-start.32) | collective-permute-done | bytes 627232 | tf_op jit(solution)/shard_map/ppermute | solution.py:23
  439.3 6.2 %shard_map.193 = bf16[280,2000]{1,0:T(8,128)(2,1)} custom-call(s32[8]{0:T(128)S(1)} %concatenate.44.info, bf16[560,2048]{1,0:T(8,128)(2,1)S(1)} %copy-done.4, bf16[560,2048]{1,0:T(8,128)(2,1)S(1)} %collective-permute-done.14.right.got, bf16[280,2048]{1,0:T(8,128)(2,1)} %collective-permute-done.15.last), custom_call_target="tpu_custom_call" | custom-call | flops 2293760 | bytes 4587520 | tf_op jit(solution)/shard_map/pallas_call | solution.py:48
  445.5 4.6 shard_map.197
  450.8 14.6 %collective-permute-done.33 = bf16[280,1120]{1,0:T(8,128)(2,1)} collective-permute-done((bf16[280,1120]{1,0:T(8,128)(2,1)}, bf16[280,1120]{1,0:T(8,128)(2,1)}, u32[]{:S(2)}, u32[]{:S(2)}) %collective-permute-start.33) | collective-permute-done | bytes 627232 | tf_op jit(solution)/shard_map/ppermute | solution.py:23
  467.0 5.2 broadcast_select_fusion.1
  472.2 10.3 %collective-permute-done.34 = bf16[280,1120]{1,0:T(8,128)(2,1)S(1)} collective-permute-done((bf16[280,1120]{1,0:T(8,128)(2,1)S(1)}, bf16[280,1120]{1,0:T(8,128)(2,1)S(1)}, u32[]{:S(2)}, u32[]{:S(2)}) %collective-permute-start.34) | collective-permute-done | bytes 627232 | tf_op jit(solution)/shard_map/ppermute | solution.py:23
  483.7 5.9 %shard_map.198 = (f32[280,2048]{1,0:T(8,128)S(1)}, f32[8,2048]{1,0:T(8,128)S(1)}, f32[280,2]{1,0:T(8,128)S(1)}) custom-call(s32[8]{0:T(128)S(1)} %concatenate.44.info, bf16[560,2048]{1,0:T(8,128)(2,1)S(1)} %copy-done.2, bf16[560,2048]{1,0:T(8,128)(2,1)} %collective-permute-done.22.right.got, bf16[280,2048]{1,0:T(8,128)(2,1)S(1)} %collective-permute-done.23.last, ...), custom_call_target="tpu_custom_call" | custom-call | flops 5734400 | bytes 8028160 | tf_op jit(solution)/shard_map/pallas_call | solution.py:48
  508.9 4.2 shard_map.199
  513.1 9.3 %collective-permute-done.35 = bf16[560,1120]{1,0:T(8,128)(2,1)S(1)} collective-permute-done((bf16[560,1120]{1,0:T(8,128)(2,1)S(1)}, bf16[560,1120]{1,0:T(8,128)(2,1)S(1)}, u32[]{:S(2)}, u32[]{:S(2)}) %collective-permute-start.35) | collective-permute-done | bytes 1254432 | tf_op jit(solution)/shard_map/ppermute | solution.py:23
  (253 shorter events, 137.7 us)
Async XLA Ops:
  0.7 28.6 %collective-permute-start.1 = (bf16[280,2000]{1,0:T(8,128)(2,1)}, bf16[280,2000]{1,0:T(8,128)(2,1)}, u32[]{:S(2)}, u32[]{:S(2)}) collective-permute-start(bf16[280,2000]{1,0:T(8,128)(2,1)} %bitcast.40), channel_id=1, source_target_pairs={{0,2},{1,3},{2,0},{3,1},{4,6},{5,7},{6,4},{7,5},{8,10},{9,11},{10,... | collective-permute-start | bytes 3360008 | tf_op jit(solution)/shard_map/ppermute | solution.py:23
  3.7 35.0 %collective-permute-start = (bf16[280,2000]{1,0:T(8,128)(2,1)}, bf16[280,2000]{1,0:T(8,128)(2,1)}, u32[]{:S(2)}, u32[]{:S(2)}) collective-permute-start(bf16[280,2000]{1,0:T(8,128)(2,1)} %bitcast.41), channel_id=1, source_target_pairs={{0,1},{1,0},{2,3},{3,2},{4,5},{5,4},{6,7},{7,6},{8,9},{9,8},{10,11... | collective-permute-start | bytes 3360008 | tf_op jit(solution)/shard_map/ppermute | solution.py:23
  78.8 28.2 %collective-permute-start.7 = (bf16[1120,512]{1,0:T(8,128)(2,1)S(1)}, bf16[1120,512]{1,0:T(8,128)(2,1)S(1)}, u32[]{:S(2)}, u32[]{:S(2)}) collective-permute-start(bf16[1120,512]{1,0:T(8,128)(2,1)S(1)} %shard_map.187), channel_id=1, source_target_pairs={{0,2},{1,3},{2,0},{3,1},{4,6},{5,7},{6,4},{7,5},{8,10},{9,11},{10,... | collective-permute-start | bytes 3440648 | tf_op jit(solution)/shard_map/ppermute | solution.py:23
  80.5 51.0 %collective-permute-start.11 = (bf16[280,2000]{1,0:T(8,128)(2,1)S(1)}, bf16[280,2000]{1,0:T(8,128)(2,1)S(1)}, u32[]{:S(2)}, u32[]{:S(2)}) collective-permute-start(bf16[280,2000]{1,0:T(8,128)(2,1)S(1)} %bitcast.47), channel_id=1, source_target_pairs={{0,2},{1,3},{2,0},{3,1},{4,6},{5,7},{6,4},{7,5},{8,10},{9,11},{10,... | collective-permute-start | bytes 3360008 | tf_op jit(solution)/shard_map/ppermute | solution.py:23
  114.3 41.3 %collective-permute-start.8 = (bf16[1120,512]{1,0:T(8,128)(2,1)}, bf16[1120,512]{1,0:T(8,128)(2,1)}, u32[]{:S(2)}, u32[]{:S(2)}) collective-permute-start(bf16[1120,512]{1,0:T(8,128)(2,1)} %get-tuple-element.44.n_one), channel_id=1, source_target_pairs={{0,2},{1,3},{2,0},{3,1},{4,6},{5,7},{6,4},{7,5},{8,10},{9,11},{10,... | collective-permute-start | bytes 3440648 | tf_op jit(solution)/shard_map/ppermute | solution.py:23
  116.0 56.4 %collective-permute-start.13 = (bf16[1120,512]{1,0:T(8,128)(2,1)}, bf16[1120,512]{1,0:T(8,128)(2,1)}, u32[]{:S(2)}, u32[]{:S(2)}) collective-permute-start(bf16[1120,512]{1,0:T(8,128)(2,1)} %get-tuple-element.44.n_one), channel_id=1, source_target_pairs={{0,1},{1,0},{2,3},{3,2},{4,5},{5,4},{6,7},{7,6},{8,9},{9,8},{10,11... | collective-permute-start | bytes 3440648 | tf_op jit(solution)/shard_map/ppermute | solution.py:23
  116.0 48.1 %collective-permute-start.10 = (bf16[280,2000]{1,0:T(8,128)(2,1)S(1)}, bf16[280,2000]{1,0:T(8,128)(2,1)}, u32[]{:S(2)}, u32[]{:S(2)}) collective-permute-start(bf16[280,2000]{1,0:T(8,128)(2,1)S(1)} %bitcast.48), channel_id=1, source_target_pairs={{0,1},{1,0},{2,3},{3,2},{4,5},{5,4},{6,7},{7,6},{8,9},{9,8},{10,11... | collective-permute-start | bytes 3360008 | tf_op jit(solution)/shard_map/ppermute | solution.py:23
  131.5 32.6 %collective-permute-start.12 = (bf16[280,2000]{1,0:T(8,128)(2,1)S(1)}, bf16[280,2000]{1,0:T(8,128)(2,1)}, u32[]{:S(2)}, u32[]{:S(2)}) collective-permute-start(bf16[280,2000]{1,0:T(8,128)(2,1)S(1)} %collective-permute-done.11.far), channel_id=1, source_target_pairs={{0,1},{1,0},{2,3},{3,2},{4,5},{5,4},{6,7},{7,6},{8,9},{9,8},{10,11... | collective-permute-start | bytes 3360008 | tf_op jit(solution)/shard_map/ppermute | solution.py:23
  155.6 39.3 %collective-permute-start.9 = (bf16[1120,512]{1,0:T(8,128)(2,1)}, bf16[1120,512]{1,0:T(8,128)(2,1)}, u32[]{:S(2)}, u32[]{:S(2)}) collective-permute-start(bf16[1120,512]{1,0:T(8,128)(2,1)} %collective-permute-done.8.n_one), channel_id=1, source_target_pairs={{0,1},{1,0},{2,3},{3,2},{4,5},{5,4},{6,7},{7,6},{8,9},{9,8},{10,11... | collective-permute-start | bytes 3440648 | tf_op jit(solution)/shard_map/ppermute | solution.py:23
  222.9 31.5 %collective-permute-start.36 = (bf16[560,1120]{1,0:T(8,128)(2,1)}, bf16[560,1120]{1,0:T(8,128)(2,1)}, u32[]{:S(2)}, u32[]{:S(2)}) collective-permute-start(bf16[560,1120]{1,0:T(8,128)(2,1)} %constant_dynamic-slice_fusion.3), channel_id=1, source_target_pairs={{0,4},{4,0},{8,12},{12,8},{16,20},{20,16},{24,28},{28,24},{1,5},{5... | collective-permute-start | bytes 3763208 | tf_op jit(solution)/shard_map/ppermute | solution.py:23
  231.1 50.0 %collective-permute-start.41 = (bf16[560,1120]{1,0:T(8,128)(2,1)}, bf16[560,1120]{1,0:T(8,128)(2,1)}, u32[]{:S(2)}, u32[]{:S(2)}) collective-permute-start(bf16[560,1120]{1,0:T(8,128)(2,1)} %constant_dynamic-slice_fusion.1), channel_id=1, source_target_pairs={{0,4},{4,0},{8,12},{12,8},{16,20},{20,16},{24,28},{28,24},{1,5},{5... | collective-permute-start | bytes 3763208 | tf_op jit(solution)/shard_map/ppermute | solution.py:23
  232.6 25.8 %collective-permute-start.16 = (bf16[1120,512]{1,0:T(8,128)(2,1)}, bf16[1120,512]{1,0:T(8,128)(2,1)}, u32[]{:S(2)}, u32[]{:S(2)}) collective-permute-start(bf16[1120,512]{1,0:T(8,128)(2,1)} %get-tuple-element.53), channel_id=1, source_target_pairs={{0,1},{1,0},{2,3},{3,2},{4,5},{5,4},{6,7},{7,6},{8,9},{9,8},{10,11... | collective-permute-start | bytes 3440648 | tf_op jit(solution)/shard_map/ppermute | solution.py:23
  234.7 27.8 %collective-permute-start.18 = (bf16[1120,512]{1,0:T(8,128)(2,1)}, bf16[1120,512]{1,0:T(8,128)(2,1)}, u32[]{:S(2)}, u32[]{:S(2)}) collective-permute-start(bf16[1120,512]{1,0:T(8,128)(2,1)} %shard_map.194), channel_id=1, source_target_pairs={{0,2},{1,3},{2,0},{3,1},{4,6},{5,7},{6,4},{7,5},{8,10},{9,11},{10,... | collective-permute-start | bytes 3440648 | tf_op jit(solution)/shard_map/ppermute | solution.py:23
  245.5 61.7 %collective-permute-start.14 = (bf16[560,2048]{1,0:T(8,128)(2,1)}, bf16[560,2048]{1,0:T(8,128)(2,1)S(1)}, u32[]{:S(2)}, u32[]{:S(2)}) collective-permute-start(bf16[560,2048]{1,0:T(8,128)(2,1)} %get-tuple-element.51), channel_id=1, source_target_pairs={{0,1},{1,0},{2,3},{3,2},{4,5},{5,4},{6,7},{7,6},{8,9},{9,8},{10,11... | collective-permute-start | bytes 6881288 | tf_op jit(solution)/shard_map/ppermute | solution.py:23
  256.5 29.0 %collective-permute-start.37 = (bf16[280,1120]{1,0:T(8,128)(2,1)S(1)}, bf16[280,1120]{1,0:T(8,128)(2,1)S(1)}, u32[]{:S(2)}, u32[]{:S(2)}) collective-permute-start(bf16[280,1120]{1,0:T(8,128)(2,1)S(1)} %constant_dynamic-slice_fusion.2), channel_id=1, source_target_pairs={{0,8},{4,12},{8,0},{12,4},{16,24},{20,28},{24,16},{28,20},{1,9},{5... | collective-permute-start | bytes 1881608 | tf_op jit(solution)/shard_map/ppermute | solution.py:23
  270.9 27.0 %collective-permute-start.20 = (bf16[1120,512]{1,0:T(8,128)(2,1)}, bf16[1120,512]{1,0:T(8,128)(2,1)}, u32[]{:S(2)}, u32[]{:S(2)}) collective-permute-start(bf16[1120,512]{1,0:T(8,128)(2,1)} %get-tuple-element.57.own), channel_id=1, source_target_pairs={{0,2},{1,3},{2,0},{3,1},{4,6},{5,7},{6,4},{7,5},{8,10},{9,11},{10,... | collective-permute-start | bytes 3440648 | tf_op jit(solution)/shard_map/ppermute | solution.py:23
  283.7 21.2 %collective-permute-start.42 = (bf16[280,1120]{1,0:T(8,128)(2,1)}, bf16[280,1120]{1,0:T(8,128)(2,1)}, u32[]{:S(2)}, u32[]{:S(2)}) collective-permute-start(bf16[280,1120]{1,0:T(8,128)(2,1)} %constant_dynamic-slice_fusion), channel_id=1, source_target_pairs={{0,8},{4,12},{8,0},{12,4},{16,24},{20,28},{24,16},{28,20},{1,9},{5... | collective-permute-start | bytes 1881608 | tf_op jit(solution)/shard_map/ppermute | solution.py:23
  286.5 46.3 %collective-permute-start.38 = (bf16[280,1120]{1,0:T(8,128)(2,1)}, bf16[280,1120]{1,0:T(8,128)(2,1)}, u32[]{:S(2)}, u32[]{:S(2)}) collective-permute-start(bf16[280,1120]{1,0:T(8,128)(2,1)} %add_convert_fusion.6), channel_id=1, source_target_pairs={{0,16},{4,20},{8,24},{12,28},{16,0},{20,4},{24,8},{28,12},{1,17},{... | collective-permute-start | bytes 1881608 | tf_op jit(solution)/shard_map/ppermute | solution.py:23
  286.5 49.2 %collective-permute-start.19 = (bf16[1120,512]{1,0:T(8,128)(2,1)}, bf16[1120,512]{1,0:T(8,128)(2,1)}, u32[]{:S(2)}, u32[]{:S(2)}) collective-permute-start(bf16[1120,512]{1,0:T(8,128)(2,1)} %get-tuple-element.57.own), channel_id=1, source_target_pairs={{0,1},{1,0},{2,3},{3,2},{4,5},{5,4},{6,7},{7,6},{8,9},{9,8},{10,11... | collective-permute-start | bytes 3440648 | tf_op jit(solution)/shard_map/ppermute | solution.py:23
  297.9 37.9 %collective-permute-start.21 = (bf16[1120,512]{1,0:T(8,128)(2,1)}, bf16[1120,512]{1,0:T(8,128)(2,1)}, u32[]{:S(2)}, u32[]{:S(2)}) collective-permute-start(bf16[1120,512]{1,0:T(8,128)(2,1)} %collective-permute-done.20.far), channel_id=1, source_target_pairs={{0,1},{1,0},{2,3},{3,2},{4,5},{5,4},{6,7},{7,6},{8,9},{9,8},{10,11... | collective-permute-start | bytes 3440648 | tf_op jit(solution)/shard_map/ppermute | solution.py:23
  307.2 75.8 %collective-permute-start.43 = (bf16[280,1120]{1,0:T(8,128)(2,1)}, bf16[280,1120]{1,0:T(8,128)(2,1)}, u32[]{:S(2)}, u32[]{:S(2)}) collective-permute-start(bf16[280,1120]{1,0:T(8,128)(2,1)} %add_convert_fusion.4), channel_id=1, source_target_pairs={{0,16},{4,20},{8,24},{12,28},{16,0},{20,4},{24,8},{28,12},{1,17},{... | collective-permute-start | bytes 1881608 | tf_op jit(solution)/shard_map/ppermute | solution.py:23
  314.6 122.9 %collective-permute-start.15 = (bf16[280,2048]{1,0:T(8,128)(2,1)}, bf16[280,2048]{1,0:T(8,128)(2,1)}, u32[]{:S(2)}, u32[]{:S(2)}) collective-permute-start(bf16[280,2048]{1,0:T(8,128)(2,1)} %shard_map.192), channel_id=1, source_target_pairs={{0,2},{1,3},{2,0},{3,1},{4,6},{5,7},{6,4},{7,5},{8,10},{9,11},{10,... | collective-permute-start | bytes 3440648 | tf_op jit(solution)/shard_map/ppermute | solution.py:23
  332.9 101.1 %collective-permute-start.27 = (f32[1120,2]{0,1:T(2,128)S(1)}, f32[1120,2]{0,1:T(2,128)S(1)}, u32[]{:S(2)}, u32[]{:S(2)}) collective-permute-start(f32[1120,2]{0,1:T(2,128)S(1)} %copy.65), channel_id=1, source_target_pairs={{0,2},{1,3},{2,0},{3,1},{4,6},{5,7},{6,4},{7,5},{8,10},{9,11},{10,... | collective-permute-start | bytes 26888 | tf_op jit(solution)/shard_map/ppermute | solution.py:23
  335.7 50.8 %collective-permute-start.39 = (bf16[280,1120]{1,0:T(8,128)(2,1)S(1)}, bf16[280,1120]{1,0:T(8,128)(2,1)S(1)}, u32[]{:S(2)}, u32[]{:S(2)}) collective-permute-start(bf16[280,1120]{1,0:T(8,128)(2,1)S(1)} %add_convert_fusion.5), channel_id=1, source_target_pairs={{0,8},{4,12},{8,0},{12,4},{16,24},{20,28},{24,16},{28,20},{1,9},{5... | collective-permute-start | bytes 1881608 | tf_op jit(solution)/shard_map/ppermute | solution.py:23
  382.9 31.3 %collective-permute-start.31 = (bf16[560,1120]{1,0:T(8,128)(2,1)S(1)}, bf16[560,1120]{1,0:T(8,128)(2,1)S(1)}, u32[]{:S(2)}, u32[]{:S(2)}) collective-permute-start(bf16[560,1120]{1,0:T(8,128)(2,1)S(1)} %fusion.18), channel_id=1, source_target_pairs={{0,4},{4,0},{8,12},{12,8},{16,20},{20,16},{24,28},{28,24},{1,5},{5... | collective-permute-start | bytes 3763208 | tf_op jit(solution)/shard_map/ppermute | solution.py:23
  384.4 31.2 %collective-permute-start.44 = (bf16[280,1120]{1,0:T(8,128)(2,1)S(1)}, bf16[280,1120]{1,0:T(8,128)(2,1)S(1)}, u32[]{:S(2)}, u32[]{:S(2)}) collective-permute-start(bf16[280,1120]{1,0:T(8,128)(2,1)S(1)} %add_convert_fusion.3), channel_id=1, source_target_pairs={{0,8},{4,12},{8,0},{12,4},{16,24},{20,28},{24,16},{28,20},{1,9},{5... | collective-permute-start | bytes 1881608 | tf_op jit(solution)/shard_map/ppermute | solution.py:23
  387.9 79.1 %collective-permute-start.40 = (bf16[560,1120]{1,0:T(8,128)(2,1)}, bf16[560,1120]{1,0:T(8,128)(2,1)}, u32[]{:S(2)}, u32[]{:S(2)}) collective-permute-start(bf16[560,1120]{1,0:T(8,128)(2,1)} %pad_maximum_fusion.4), channel_id=1, source_target_pairs={{0,4},{4,0},{8,12},{12,8},{16,20},{20,16},{24,28},{28,24},{1,5},{5... | collective-permute-start | bytes 3763208 | tf_op jit(solution)/shard_map/ppermute | solution.py:23
  414.3 31.2 %collective-permute-start.22 = (bf16[560,2048]{1,0:T(8,128)(2,1)}, bf16[560,2048]{1,0:T(8,128)(2,1)}, u32[]{:S(2)}, u32[]{:S(2)}) collective-permute-start(bf16[560,2048]{1,0:T(8,128)(2,1)} %get-tuple-element.61), channel_id=1, source_target_pairs={{0,1},{1,0},{2,3},{3,2},{4,5},{5,4},{6,7},{7,6},{8,9},{9,8},{10,11... | collective-permute-start | bytes 6881288 | tf_op jit(solution)/shard_map/ppermute | solution.py:23
  432.9 34.0 %collective-permute-start.45 = (bf16[560,1120]{1,0:T(8,128)(2,1)}, bf16[560,1120]{1,0:T(8,128)(2,1)}, u32[]{:S(2)}, u32[]{:S(2)}) collective-permute-start(bf16[560,1120]{1,0:T(8,128)(2,1)} %pad_maximum_fusion.5), channel_id=1, source_target_pairs={{0,4},{4,0},{8,12},{12,8},{16,20},{20,16},{24,28},{28,24},{1,5},{5... | collective-permute-start | bytes 3763208 | tf_op jit(solution)/shard_map/ppermute | solution.py:23
  433.9 31.5 %collective-permute-start.33 = (bf16[280,1120]{1,0:T(8,128)(2,1)}, bf16[280,1120]{1,0:T(8,128)(2,1)}, u32[]{:S(2)}, u32[]{:S(2)}) collective-permute-start(bf16[280,1120]{1,0:T(8,128)(2,1)} %add_convert_fusion.8), channel_id=1, source_target_pairs={{0,16},{4,20},{8,24},{12,28},{16,0},{20,4},{24,8},{28,12},{1,17},{... | collective-permute-start | bytes 1881608 | tf_op jit(solution)/shard_map/ppermute | solution.py:23
  450.1 33.5 %collective-permute-start.23 = (bf16[280,2048]{1,0:T(8,128)(2,1)S(1)}, bf16[280,2048]{1,0:T(8,128)(2,1)S(1)}, u32[]{:S(2)}, u32[]{:S(2)}) collective-permute-start(bf16[280,2048]{1,0:T(8,128)(2,1)S(1)} %shard_map.197), channel_id=1, source_target_pairs={{0,2},{1,3},{2,0},{3,1},{4,6},{5,7},{6,4},{7,5},{8,10},{9,11},{10,... | collective-permute-start | bytes 3440648 | tf_op jit(solution)/shard_map/ppermute | solution.py:23
  494.3 28.1 %collective-permute-start.35 = (bf16[560,1120]{1,0:T(8,128)(2,1)S(1)}, bf16[560,1120]{1,0:T(8,128)(2,1)S(1)}, u32[]{:S(2)}, u32[]{:S(2)}) collective-permute-start(bf16[560,1120]{1,0:T(8,128)(2,1)S(1)} %pad_maximum_fusion.3), channel_id=1, source_target_pairs={{0,4},{4,0},{8,12},{12,8},{16,20},{20,16},{24,28},{28,24},{1,5},{5... | collective-permute-start | bytes 3763208 | tf_op jit(solution)/shard_map/ppermute | solution.py:23
  (65 other events, 652.7 us)
